TPU v7x, 128 devices: a whole 4x4x4 slice. The times are simulated.
128 devices in a mesh: sx: 8 (over z, core), sy: 16 (over y, x).
Axes of the slice: x: 4, y: 4, z: 4, core: 2. Of those that a mesh axis runs over, the one named last changes fastest.
Arguments:
- grid_points: float32 [3, 262144], P(None, ('sx', 'sy')), may hold values from 0 to 16
- weighted_density: float32 [262144], P(('sx', 'sy')), may hold values from -0.15 to 0.15
- point_slot: int32 [262144], P(('sx', 'sy')), may hold values from 0 to 127, as said below
- near_slot: int32 [2048, 64], P(('sx', 'sy')), may hold values from 0 to 127, as said below
- slot_atom: int32 [16384], replicated, may hold values from 0 to 2047, as said below
- atom_pos: float32 [3, 2048], replicated, may hold values from 0 to 16
- decay_rates: float32 [128], replicated, may hold values from 0.5 to 2
- green: float32 [7, 128, 128], replicated, may hold values from -0.5 to 0.5
- moment_table: float32 [3, 128], replicated, may hold values from 0.5 to 5
Outputs:
- potential: float32 [262144], P(('sx', 'sy'))
Inputs may be any that keep to these rules, and one draw needn't show every extreme that they name: `slot_atom`: atoms are owned in ranges in device order: devices below 32 own 2 * 16 atoms each, those below 64 own 16, the rest 16 // 2; the 128 atoms listed by one device are distinct; at most 2 of them have one owner, and in every draw one owner has exactly 2 atoms in every device's list. `near_slot`: the 64 entries of one batch are distinct. `point_slot`: each point's entry is one of its batch's near entries.
All inputs are finite; a program needn't handle non-finite values.
Results may differ from a plain program's by a relative error of at most 0.004.
Values may be sent and summed in bfloat16 or wider, within the bound.
A program may use at most 64 MiB of HBM per device.

v0:
```python
import math

import jax
import jax.numpy as jnp
import numpy as np
from jax import lax
from jax.sharding import PartitionSpec as P

HARM = 49
NRAD = 128
OWN_AVG = 16
OWN = 32


def harmonic_table(comp_x, comp_y, comp_z, top_degree):
    square = comp_x * comp_x + comp_y * comp_y + comp_z * comp_z
    cosines = [jnp.ones_like(comp_x)]
    sine_terms = [jnp.zeros_like(comp_x)]
    for m in range(1, top_degree + 1):
        cosines.append(cosines[m - 1] * comp_x - sine_terms[m - 1] * comp_y)
        sine_terms.append(cosines[m - 1] * comp_y + sine_terms[m - 1] * comp_x)
    legendre = {}
    for m in range(top_degree + 1):
        legendre[m, m] = float(math.prod(range(1, 2 * m, 2))) * cosines[0]
        if m + 1 <= top_degree:
            legendre[m + 1, m] = (2 * m + 1) * comp_z * legendre[m, m]
        for l in range(m + 2, top_degree + 1):
            legendre[l, m] = (
                (2 * l - 1) * comp_z * legendre[l - 1, m]
                - (l + m - 1) * square * legendre[l - 2, m]
            ) / (l - m)
    stacked = []
    for l in range(top_degree + 1):
        for m in range(l + 1):
            factor = math.sqrt(
                (2 * l + 1) / (4 * math.pi) * math.factorial(l - m) / math.factorial(l + m)
            )
            if m == 0:
                stacked.append(factor * legendre[l, 0])
            else:
                factor = factor * math.sqrt(2.0)
                stacked.append(factor * legendre[l, m] * cosines[m])
                stacked.append(factor * legendre[l, m] * sine_terms[m])
    return jnp.stack(stacked)


def soft_geometry(delta):
    distance = jnp.sqrt(jnp.sum(delta * delta, axis=0) + 1.0)
    return (distance, delta / distance)


def shell_layout(decay_rates):
    count = decay_rates.shape[0]
    spacing = 27.0 / (count - 1)
    centres = 1.0 + spacing * jnp.arange(count).astype(decay_rates.dtype)
    return (centres, spacing)


def shell_values(distance, rates, centres, spacing):
    offset = (distance - centres) / spacing
    return jnp.exp(-rates * offset * offset)


def project_points(points, density, slot_of_point, atom_list, atom_pos, decay_rates):
    listed = atom_list.shape[0]
    atom_ids = atom_list[slot_of_point]
    delta = points - atom_pos[:, atom_ids]
    distance, unit_vec = soft_geometry(delta)
    harmonics = harmonic_table(unit_vec[0], unit_vec[1], unit_vec[2], 6)
    projected = (density[None, :] * harmonics).astype(jnp.bfloat16)
    centres, spacing = shell_layout(decay_rates)
    radial = shell_values(
        distance[None, :], decay_rates[:, None], centres[:, None], spacing
    ).astype(jnp.bfloat16)
    onehot = (slot_of_point[None, :] == jnp.arange(listed)[:, None]).astype(jnp.bfloat16)
    weighted = onehot[:, None, :] * projected[None, :, :]
    terms = jnp.einsum("tip,kp->tik", weighted, radial, preferred_element_type=jnp.float32)
    return terms.reshape(listed, -1)


def apply_green(coefficients, green):
    pieces = []
    for l in range(7):
        pieces.append(
            jnp.einsum(
                "aik,kn->ain",
                coefficients[:, l * l : (l + 1) * (l + 1)],
                green[l],
                precision=lax.Precision.HIGHEST,
            )
        )
    return jnp.concatenate(pieces, axis=1)


def low_moments(coefficients, moment_table):
    degrees = np.array([0, 1, 1, 1, 2, 2, 2, 2, 2])
    table = moment_table[degrees]
    return jnp.einsum("aik,ik->ia", coefficients[:, :9], table, precision=lax.Precision.HIGHEST)


def near_field(points, near_ids, near_coef, atom_pos, decay_rates):
    batches = near_ids.shape[0]
    batch_pts = points.shape[1] // batches
    grouped = points.reshape(3, batches, batch_pts)
    delta = grouped[:, :, None, :] - atom_pos[:, near_ids][..., None]
    distance, unit_vec = soft_geometry(delta)
    harmonics = harmonic_table(unit_vec[0], unit_vec[1], unit_vec[2], 6)
    centres, spacing = shell_layout(decay_rates)
    radial = shell_values(
        distance[:, :, None, :],
        decay_rates[None, None, :, None],
        centres[None, None, :, None],
        spacing,
    ).astype(jnp.bfloat16)
    values = jnp.einsum("bjik,bjkp->bjip", near_coef, radial, preferred_element_type=jnp.float32)
    return jnp.sum(values * jnp.moveaxis(harmonics, 0, 2), axis=(1, 2)).reshape(-1)


def far_field(points, near_ids, moments, atom_pos):
    batches = near_ids.shape[0]
    batch_pts = points.shape[1] // batches
    grouped = jnp.moveaxis(points.reshape(3, batches, batch_pts), 1, 0)
    atom_index = jnp.arange(atom_pos.shape[1])

    def one_batch(inputs):
        coords, ids = inputs
        delta = coords[:, :, None] - atom_pos[:, None, :]
        distance, unit_vec = soft_geometry(delta)
        harmonics = harmonic_table(unit_vec[0], unit_vec[1], unit_vec[2], 2)
        inverse = 1.0 / distance
        keep = 1.0 - jnp.sum((ids[:, None] == atom_index[None, :]).astype(jnp.float32), axis=0)
        scaled = moments * keep[None, :]
        total = harmonics[0] * scaled[0][None, :] * inverse
        total = total + jnp.sum(harmonics[1:4] * scaled[1:4, None, :], axis=0) * inverse * inverse
        total = (
            total
            + jnp.sum(harmonics[4:9] * scaled[4:9, None, :], axis=0) * inverse * inverse * inverse
        )
        return jnp.sum(total, axis=1)

    return lax.map(one_batch, (grouped, near_ids)).reshape(-1)


def per_device(
    grid_points,
    weighted_density,
    point_slot,
    near_slot,
    slot_atom,
    atom_pos,
    decay_rates,
    green,
    moment_table,
):
    count_x = lax.axis_size("sx")
    count_y = lax.axis_size("sy")
    devices = count_x * count_y
    myself = lax.axis_index("sx") * count_y + lax.axis_index("sy")
    all_lists = slot_atom.reshape(devices, -1)
    listed = all_lists.shape[1]
    capacity = 2 * listed // devices
    total_atoms = atom_pos.shape[1]
    my_list = all_lists[myself]
    batches = near_slot.shape[0]
    near_count = near_slot.shape[1]
    batch_pts = grid_points.shape[1] // batches
    block = math.gcd(batches, 4)
    groups = batches // block
    group_points = jnp.moveaxis(grid_points.reshape(3, groups, block * batch_pts), 1, 0)
    group_density = weighted_density.reshape(groups, block * batch_pts)
    group_slots = point_slot.reshape(groups, block * batch_pts)
    group_near = near_slot.reshape(groups, block, near_count)
    width = HARM * NRAD

    def project_step(total, inputs):
        points, density, slot_of_point = inputs
        return (
            total + project_points(points, density, slot_of_point, my_list, atom_pos, decay_rates),
            None,
        )

    summed, unused = lax.scan(
        project_step,
        jnp.zeros((listed, width), jnp.float32),
        (group_points, group_density, group_slots),
    )
    partial_value = summed.astype(jnp.bfloat16)
    owner_ids = jnp.arange(devices)
    counts = jnp.where(
        owner_ids < devices // 4,
        2 * OWN_AVG,
        jnp.where(owner_ids < devices // 2, OWN_AVG, OWN_AVG // 2),
    ).astype(jnp.int32)
    range_ends = jnp.cumsum(counts)
    starts = range_ends - counts
    atom_index = jnp.arange(total_atoms)
    owner = jnp.sum((range_ends[None, :] <= atom_index[:, None]).astype(jnp.int32), axis=1)
    owners_all = owner[all_lists]
    my_dest = owners_all[myself]
    slot_index = jnp.arange(listed)
    same_owner = (my_dest[:, None] == my_dest[None, :]) & (
        slot_index[None, :] < slot_index[:, None]
    )
    earlier = jnp.sum(same_owner.astype(jnp.int32), axis=1)
    send_row = my_dest * capacity + earlier
    packing = (jnp.arange(devices * capacity)[:, None] == send_row[None, :]).astype(jnp.bfloat16)
    outgoing = jnp.dot(packing, partial_value, preferred_element_type=jnp.float32).astype(
        jnp.bfloat16
    )
    mine = owners_all == myself
    recv_rank = jnp.cumsum(mine.astype(jnp.int32), axis=1) - 1
    target = jnp.where(mine, owner_ids[:, None] * capacity + recv_rank, devices * capacity)
    local_ids = jnp.where(mine, all_lists - starts[myself], OWN)
    row_owned = (
        jnp.full((devices * capacity + 1,), OWN, jnp.int32)
        .at[target.reshape(-1)]
        .set(local_ids.reshape(-1))[: devices * capacity]
    )
    incoming = lax.all_to_all(outgoing, ("sx", "sy"), split_axis=0, concat_axis=0, tiled=True)
    selector = (row_owned[None, :] == jnp.arange(OWN)[:, None]).astype(jnp.bfloat16)
    coeff_own = jnp.dot(selector, incoming, preferred_element_type=jnp.float32).reshape(
        OWN, HARM, NRAD
    )
    pot_own = apply_green(coeff_own, green).astype(jnp.bfloat16).reshape(OWN, width)
    moments_own = low_moments(coeff_own, moment_table)
    reply = jnp.dot(selector.T, pot_own, preferred_element_type=jnp.float32).astype(jnp.bfloat16)
    returned = lax.all_to_all(reply, ("sx", "sy"), split_axis=0, concat_axis=0, tiled=True)
    gathered = lax.all_gather(moments_own, ("sx", "sy"), axis=1, tiled=True)
    column = owner * OWN + atom_index - starts[owner]
    moments_all = gathered[:, column]
    slot_pot = jnp.dot(packing.T, returned, preferred_element_type=jnp.float32).astype(jnp.bfloat16)
    near_ids = my_list[near_slot]
    group_ids = near_ids.reshape(groups, block, near_count)
    list_index = jnp.arange(listed)

    def near_group(inputs):
        points, ids, near_list = inputs
        picker = (near_list[:, :, None] == list_index[None, None, :]).astype(jnp.bfloat16)
        near_coef = jnp.einsum(
            "bjt,tw->bjw", picker, slot_pot, preferred_element_type=jnp.float32
        ).astype(jnp.bfloat16)
        near_coef = near_coef.reshape(block, near_count, HARM, NRAD)
        return near_field(points, ids, near_coef, atom_pos, decay_rates)

    near_part = lax.map(near_group, (group_points, group_ids, group_near)).reshape(-1)
    far_part = far_field(grid_points, near_ids, moments_all, atom_pos)
    return near_part + far_part


def solution(mesh):
    return jax.shard_map(
        per_device,
        mesh=mesh,
        in_specs=(
            P(None, ("sx", "sy")),
            P(("sx", "sy")),
            P(("sx", "sy")),
            P(("sx", "sy"), None),
            P(),
            P(),
            P(),
            P(),
            P(),
        ),
        out_specs=P(("sx", "sy")),
        check_vma=False,
    )
```

profile of v0, /device:TPU:1, one launch (start us, length us, event | category | flops | bytes accessed | tf_op | source)
XLA Modules:
  0.0 600.3 jit_solution(10263275687308145965)
XLA Ops:
  1.6 90.5 %gather_fusion.3 = s32[16384]{0:T(1024)S(1)} fusion(s32[2048]{0:T(1024)S(1)} %convert_reduce_fusion.1, s32[16384]{0:T(1024)S(1)} %fusion.58), kind=kCustom, calls=%fused_computation.3 | custom fusion | bytes 196608 | tf_op jit(solution)/shard_map/gather | solution.py:198
  92.3 1.4 copy.273
  94.9 1.2 fusion.86
  96.2 83.5 %while.47 = (s32[]{:T(128)}, f32[128,6272]{0,1:T(8,128)S(1)}, s32[4,512]{1,0:T(4,128)S(1)}, f32[4,512]{1,0:T(4,128)}, f32[4,3,512]{2,1,0:T(4,128)}, /*index=5*/s...) while((s32[]{:T(128)}, f32[128,6272]{0,1:T(8,128)S(1)}, ...), condition=%wide.region_7.8_spmd.clone, body=%wide.region_5.7_spmd.clone.sunk | while | flops 827510272 | bytes 13908703 | solution.py:182
  96.8 3.3 gather_fusion.1
  100.1 2.3 gather_fusion.2
  105.4 2.9 stack.25
  109.7 4.5 fusion.142
  114.3 2.7 bitcast_add_fusion.4
  117.6 3.3 gather_fusion.1
  121.0 2.3 gather_fusion.2
  126.3 2.9 stack.25
  130.6 4.5 fusion.142
  135.1 2.7 bitcast_add_fusion.4
  138.5 3.3 gather_fusion.1
  141.9 2.3 gather_fusion.2
  147.2 2.9 stack.25
  151.5 4.5 fusion.142
  156.0 2.7 bitcast_add_fusion.4
  159.4 3.3 gather_fusion.1
  162.7 2.3 gather_fusion.2
  168.0 2.9 stack.25
  172.3 4.5 fusion.142
  176.9 2.7 bitcast_add_fusion.4
  179.6 3.3 convolution_convert_fusion.2
  183.0 7.2 %all_to_all.16 = bf16[128,2,6272]{2,1,0:T(2,128)(2,1)} reshape(bf16[256,6272]{1,0:T(8,128)(2,1)} %convolution_convert_fusion.2) | data formatting | bytes 6422528 | tf_op jit(solution)/shard_map/all_to_all | solution.py:219
  190.1 11.9 %all-to-all-start = ((bf16[128,2,6272]{2,1,0:T(2,128)(2,1)}), bf16[128,2,6272]{2,1,0:T(2,128)(2,1)}, u32[]{:S(2)}, u32[]{:S(2)}) async-start(bf16[128,2,6272]{2,1,0:T(2,128)(2,1)} %all_to_all.16), calls=%async_computation | async-start | bytes 6422528 | tf_op jit(solution)/shard_map/all_to_all | solution.py:219
  202.8 6.6 %gather_fusion.4 = s32[1024]{0:T(1024)S(1)} fusion(s32[128]{0:T(128)S(1)} %get-tuple-element.1387, s32[1024]{0:T(1024)S(1)} %get-tuple-element.976), kind=kCustom, calls=%fused_computation.4 | custom fusion | bytes 12288 | tf_op jit(solution)/shard_map/gather | solution.py:232
  210.8 60.5 %scatter_custom_fusion = s32[257]{0:T(512)S(1)} fusion(s32[16384]{0:T(1024)S(1)} %bitcast.236, s32[16384]{0:T(1024)S(1)} %subtract_select_fusion, s32[]{:T(128)} %constant.1003.clone.1), kind=kCustom, calls=%fused_computation.317 | custom fusion | bytes 1032 | tf_op jit(solution)/shard_map/scatter | solution.py:217
  271.3 12.6 %gather_fusion.6 = s32[2048]{0:T(1024)S(1)} fusion(s32[128]{0:T(128)S(1)} %fusion.85, s32[2048]{0:T(1024)S(1)} %broadcast_clamp_fusion.1), kind=kCustom, calls=%fused_computation.6 | custom fusion | bytes 24576 | tf_op jit(solution)/shard_map/gather | solution.py:229
  284.6 6.3 %all_to_all.18 = bf16[256,6272]{1,0:T(8,128)(2,1)S(1)} reshape(bf16[128,2,6272]{2,1,0:T(2,128)(2,1)} %all-to-all-done) | data formatting | bytes 6422528 | tf_op jit(solution)/shard_map/all_to_all | solution.py:219
  290.8 3.5 copy.274
  294.3 2.9 fusion.77
  306.1 2.8 all_to_all.19
  308.9 9.8 %all-to-all-start.1 = ((bf16[128,2,6272]{2,1,0:T(2,128)(2,1)}), bf16[128,2,6272]{2,1,0:T(2,128)(2,1)S(1)}, u32[]{:S(2)}, u32[]{:S(2)}) async-start(bf16[128,2,6272]{2,1,0:T(2,128)(2,1)} %all_to_all.19), calls=%async_computation.1 | async-start | bytes 6422528 | tf_op jit(solution)/shard_map/all_to_all | solution.py:227
  318.6 1.2 fusion.81
  319.9 93.8 %all-gather = f32[128,32,9]{1,2,0:T(8,128)} all-gather(f32[1,32,9]{1,2,0:T(8,128)S(1)} %bitcast.239), channel_id=1, replica_groups=mesh['sx'=8,'sy'=16] {'sx','sy'}, dimensions={0}, use_global_device_ids=true | all-gather | bytes 148608 | tf_op jit(solution)/shard_map/all_gather | solution.py:228
  413.7 3.4 copy.277
  417.1 9.2 %gather_fusion.7 = f32[2048,9]{1,0:T(8,128)} fusion(f32[9,4096]{0,1:T(8,128)} %bitcast.216, s32[2048]{0:T(1024)S(1)} %broadcast_clamp_fusion), kind=kCustom, calls=%fused_computation.7 | custom fusion | bytes 155648 | tf_op jit(solution)/shard_map/gather | solution.py:230
  426.2 1.5 copy.278
  427.8 72.1 %while.46 = (s32[]{:T(128)}, f32[16,128]{1,0:T(8,128)S(1)}, f32[16,3,128]{2,1,0:T(4,128)S(1)}, f32[3,2048]{1,0:T(4,128)S(1)}, s32[16,64]{1,0:T(8,128)S(1)}, /*index=5*/f32[9,2048]{1,0:T(8,128)S(1)}, s32[]{:T(128)}, s32[]{:T(128)}) while((s32[]{:T(128)}, f32[16,128]{1,0:T(8,128)S(1)}, f32[16,3,128]{2,1,0:T(4,128)S(1)}, ...), condition=%wide.region_18.19_spmd.clone, body=%wide.region_12.18_spmd.clone.sunk | while | flops 21122944 | bytes 44499296 | solution.py:141
  499.9 2.8 all_to_all.21
  502.7 3.7 convolution_convert_fusion.3
  506.4 93.2 %while.45 = (s32[]{:T(128)}, f32[4,512]{1,0:T(4,128)S(1)}, s32[4,4,64]{2,1,0:T(4,128)S(1)}, bf16[128,6272]{1,0:T(8,128)(2,1)}, f32[4,3,512]{2,1,0:T(4,128)S(1)},...) while((s32[]{:T(128)}, f32[4,512]{1,0:T(4,128)S(1)}, ...), condition=%wide.region_11.12_spmd.clone, body=%wide.region_8.11_spmd.clone.sunk | while | flops 861898496 | bytes 92647080 | solution.py:245
  506.5 1.9 gather_fusion
  511.6 2.7 copy-done.2
  515.3 3.1 reshape.986
  518.4 6.9 %fusion.129 = f32[4,64,49,128]{3,2,1,0:T(8,128)S(1)} fusion(bf16[4,64,49,128]{3,2,1,0:T(8,128)(2,1)} %reshape.986, f32[128]{0:T(128)S(1)} %multiply_bitcast_fusion.4, f32[128]{0:T(128)S(1)} %multiply_add_fusion.29, f32[4,64,128]{2,1,0:T(8,128)S(1)} %add_sqrt_fusion.6), kind=kOutput, calls=%fused_computation.17.clone.1 | convolution fusion | flops 432013312 | bytes 9765888 | tf_op jit(solution)/shard_map/while/body/eval_jaxpr/bjik,bjkp->bjip/dot_general | solution.py:115
  525.4 4.3 fusion.130
  529.8 1.9 gather_fusion
  534.9 2.7 copy-done.2
  538.6 3.1 reshape.986
  541.7 6.9 %fusion.129 = f32[4,64,49,128]{3,2,1,0:T(8,128)S(1)} fusion(bf16[4,64,49,128]{3,2,1,0:T(8,128)(2,1)} %reshape.986, f32[128]{0:T(128)S(1)} %multiply_bitcast_fusion.4, f32[128]{0:T(128)S(1)} %multiply_add_fusion.29, f32[4,64,128]{2,1,0:T(8,128)S(1)} %add_sqrt_fusion.6), kind=kOutput, calls=%fused_computation.17.clone.1 | convolution fusion | flops 432013312 | bytes 9765888 | tf_op jit(solution)/shard_map/while/body/eval_jaxpr/bjik,bjkp->bjip/dot_general | solution.py:115
  548.7 4.3 fusion.130
  553.1 1.9 gather_fusion
  558.2 2.7 copy-done.2
  562.0 3.1 reshape.986
  565.0 6.9 %fusion.129 = f32[4,64,49,128]{3,2,1,0:T(8,128)S(1)} fusion(bf16[4,64,49,128]{3,2,1,0:T(8,128)(2,1)} %reshape.986, f32[128]{0:T(128)S(1)} %multiply_bitcast_fusion.4, f32[128]{0:T(128)S(1)} %multiply_add_fusion.29, f32[4,64,128]{2,1,0:T(8,128)S(1)} %add_sqrt_fusion.6), kind=kOutput, calls=%fused_computation.17.clone.1 | convolution fusion | flops 432013312 | bytes 9765888 | tf_op jit(solution)/shard_map/while/body/eval_jaxpr/bjik,bjkp->bjip/dot_general | solution.py:115
  572.0 4.3 fusion.130
  576.4 1.9 gather_fusion
  581.5 2.7 copy-done.2
  585.3 3.1 reshape.986
  588.3 6.9 %fusion.129 = f32[4,64,49,128]{3,2,1,0:T(8,128)S(1)} fusion(bf16[4,64,49,128]{3,2,1,0:T(8,128)(2,1)} %reshape.986, f32[128]{0:T(128)S(1)} %multiply_bitcast_fusion.4, f32[128]{0:T(128)S(1)} %multiply_add_fusion.29, f32[4,64,128]{2,1,0:T(8,128)S(1)} %add_sqrt_fusion.6), kind=kOutput, calls=%fused_computation.17.clone.1 | convolution fusion | flops 432013312 | bytes 9765888 | tf_op jit(solution)/shard_map/while/body/eval_jaxpr/bjik,bjkp->bjip/dot_general | solution.py:115
  595.3 4.3 fusion.130
  (786 shorter events, 120.1 us)
Async XLA Ops:
  0.0 283.9 %copy-start = (f32[3,128]{1,0:T(4,128)S(1)}, f32[3,128]{1,0:T(4,128)}, u32[]{:S(2)}) copy-start(f32[3,128]{1,0:T(4,128)} %param.25) | copy-start | bytes 4612
  0.3 91.8 %copy-start.17 = (s32[128]{0:T(128)}, s32[128]{0:T(128)S(1)}, u32[]{:S(2)}) copy-start(s32[128]{0:T(128)S(1)} %reduce) | copy-start | bytes 1540
  1.5 90.8 %copy-start.5 = (f32[3,2048]{1,0:T(4,128)S(1)}, f32[3,2048]{1,0:T(4,128)}, u32[]{:S(2)}) copy-start(f32[3,2048]{1,0:T(4,128)} %param.22) | copy-start | bytes 73732
  1.5 92.2 %copy-start.20 = (f32[128]{0:T(128)S(1)}, f32[128]{0:T(128)}, u32[]{:S(2)}) copy-start(f32[128]{0:T(128)} %param.23) | copy-start | bytes 1540
  1.6 92.8 %copy-start.14 = (s32[2048]{0:T(1024)S(1)}, s32[2048]{0:T(1024)}, u32[]{:S(2)}) copy-start(s32[2048]{0:T(1024)} %param.19) | copy-start | bytes 24580
  1.6 92.8 %copy-start.15 = (f32[2048]{0:T(1024)S(1)}, f32[2048]{0:T(1024)}, u32[]{:S(2)}) copy-start(f32[2048]{0:T(1024)} %param.18) | copy-start | bytes 24580
  92.1 4.0 copy-start.8
  96.2 0.6 copy-start.12
  103.3 0.6 copy-start.10
  114.3 2.8 copy-start.13
  117.0 0.6 copy-start.12
  124.1 0.6 copy-start.10
  135.1 2.8 copy-start.13
  137.9 0.6 copy-start.12
  145.0 0.6 copy-start.10
  156.0 2.8 copy-start.13
  158.8 0.6 copy-start.12
  165.9 0.6 copy-start.10
  176.9 2.8 copy-start.13
  183.0 19.1 %copy-start.9 = (s32[16384]{0:T(1024)S(1)}, s32[16384]{0:T(1024)}, u32[]{:S(2)}) copy-start(s32[16384]{0:T(1024)} %copy-done.8) | copy-start | bytes 196612
  183.0 19.7 %copy-start.11 = (s32[16,64]{1,0:T(8,128)S(1)}, s32[16,64]{1,0:T(8,128)}, u32[]{:S(2)}) copy-start(s32[16,64]{1,0:T(8,128)} %param.20) | copy-start | bytes 12292
  183.0 19.8 %copy-start.19 = (s32[9]{0:T(128)S(1)}, s32[9]{0:T(128)}, u32[]{:S(2)}) copy-start(s32[9]{0:T(128)} %constant.1017) | copy-start | bytes 112
  190.1 19.4 %copy-start.18 = (s32[128]{0:T(128)S(1)}, s32[128]{0:T(128)}, u32[]{:S(2)}) copy-start(s32[128]{0:T(128)} %copy-done.17) | copy-start | bytes 1540
  190.1 20.0 %copy-start.7 = (s32[16384]{0:T(1024)S(1)}, s32[16384]{0:T(1024)}, u32[]{:S(2)}) copy-start(s32[16384]{0:T(1024)} %param.21) | copy-start | bytes 196612
  190.1 94.4 %all-to-all-start = ((bf16[128,2,6272]{2,1,0:T(2,128)(2,1)}), bf16[128,2,6272]{2,1,0:T(2,128)(2,1)}, u32[]{:S(2)}, u32[]{:S(2)}) async-start(bf16[128,2,6272]{2,1,0:T(2,128)(2,1)} %all_to_all.16), calls=%async_computation | async-start | bytes 6422528 | tf_op jit(solution)/shard_map/all_to_all | solution.py:219
  297.2 6.6 %copy-start.4 = (f32[32,49,128]{2,0,1:T(8,128)}, f32[32,49,128]{2,0,1:T(8,128)S(1)}, u32[]{:S(2)}) copy-start(f32[32,49,128]{2,0,1:T(8,128)S(1)} %fusion.77) | copy-start | bytes 2408452
  308.9 118.9 %copy-start.6 = (f32[4,3,512]{2,1,0:T(4,128)S(1)}, f32[4,3,512]{2,1,0:T(4,128)}, u32[]{:S(2)}) copy-start(f32[4,3,512]{2,1,0:T(4,128)} %get-tuple-element.1392) | copy-start | bytes 73732
  308.9 191.0 %all-to-all-start.1 = ((bf16[128,2,6272]{2,1,0:T(2,128)(2,1)}), bf16[128,2,6272]{2,1,0:T(2,128)(2,1)S(1)}, u32[]{:S(2)}, u32[]{:S(2)}) async-start(bf16[128,2,6272]{2,1,0:T(2,128)(2,1)} %all_to_all.19), calls=%async_computation.1 | async-start | bytes 6422528 | tf_op jit(solution)/shard_map/all_to_all | solution.py:227
  499.9 2.8 copy-start.16
  499.9 6.5 %copy-start.21 = (f32[1,1,128,1]{2,3,1,0:T(1,128)S(1)}, f32[1,1,128,1]{2,3,1,0:T(1,128)}, u32[]{:S(2)}) copy-start(f32[1,1,128,1]{2,3,1,0:T(1,128)} %get-tuple-element.1340) | copy-start | bytes 1540
  510.0 4.3 copy-start.3
  511.6 2.7 copy-start.2
  533.3 4.3 copy-start.3
  534.9 2.7 copy-start.2
  556.6 4.3 copy-start.3
  558.2 2.7 copy-start.2
  579.9 4.3 copy-start.3
  581.5 2.7 copy-start.2
  599.6 0.7 copy-start.1
where the time goes:
time: 604 us; the launch traced here: 600 us
  local copies, waits for them, and re-layouts  286 us (47%)
  other arithmetic  124 us (21%)
  blocking collectives  93.8 us (16%)
  matrix products  70.1 us (12%)
  starting transfers between devices  21.7 us (4%)
    all_gather x1, blocking collectives, per_device(): gathered = lax.all_gather(moments_own, ('sx', 'sy'), axis=1, tiled=True)  93.8 us
    gather x2, local copies, waits for them, and re-layouts, per_device(): owners_all = owner[all_lists]  90.6 us
    scatter x1, local copies, waits for them, and re-layouts, per_device(): row_owned = jnp.full((devices * capacity + 1,), OWN, jnp.int32).at[target...  60.5 us
    dot_general x4, matrix products, near_field(): jnp.einsum('bjik,bjkp->bjip', near_coef, radial, preferred_element_type=j...  27.8 us
    while x236, other arithmetic  21 us
    dot_general x4, matrix products, project_points(): jnp.einsum('tip,kp->tik', weighted, radial, preferred_element_type=jnp.fl...  18.2 us
    reduce_sum x4, other arithmetic, near_field(): jnp.sum(values * jnp.moveaxis(harmonics, 0, 2), axis=(1, 2)).reshape(-1)  17.1 us
    all_to_all x3, local copies, waits for them, and re-layouts, per_device(): lax.all_to_all(outgoing, ('sx', 'sy'), split_axis=0, concat_axis=0, tiled...  16.9 us
  transfers between devices with their start and end apart: 2, of which 0 were waited for; matrix products, arithmetic and copies ran while one was open for 28% of the time, Pallas kernels for 0%

commit v1 on v0

--- a/solution.py
+++ b/solution.py
@@ -4,6 +4,8 @@
 import jax.numpy as jnp
 import numpy as np
 from jax import lax
+from jax.experimental import pallas as pl
+from jax.experimental.pallas import tpu as pltpu
 from jax.sharding import PartitionSpec as P
 
 HARM = 49
@@ -98,47 +100,272 @@
     return jnp.einsum("aik,ik->ia", coefficients[:, :9], table, precision=lax.Precision.HIGHEST)
 
 
-def near_field(points, near_ids, near_coef, atom_pos, decay_rates):
-    batches = near_ids.shape[0]
-    batch_pts = points.shape[1] // batches
-    grouped = points.reshape(3, batches, batch_pts)
-    delta = grouped[:, :, None, :] - atom_pos[:, near_ids][..., None]
-    distance, unit_vec = soft_geometry(delta)
-    harmonics = harmonic_table(unit_vec[0], unit_vec[1], unit_vec[2], 6)
+HP = 64
+YR = 56
+
+
+def y_factor(l, m):
+    factor = math.sqrt(
+        (2 * l + 1) / (4 * math.pi) * math.factorial(l - m) / math.factorial(l + m)
+    )
+    return factor if m == 0 else factor * math.sqrt(2.0)
+
+
+def harmonic_rows(x, y, z, top, emit):
+    square = x * x + y * y + z * z
+    cos_m, sin_m = None, None
+    for m in range(top + 1):
+        if m == 1:
+            cos_m, sin_m = x, y
+        elif m > 1:
+            cos_m, sin_m = cos_m * x - sin_m * y, cos_m * y + sin_m * x
+        double = float(math.prod(range(1, 2 * m, 2)))
+        ladder = {}
+        for l in range(m, top + 1):
+            if l == m + 1:
+                ladder[l] = z * float(2 * m + 1)
+            elif l == m + 2:
+                ladder[l] = z * ladder[l - 1] * ((2 * l - 1) / 2) - square * ((l + m - 1) / 2)
+            elif l > m + 2:
+                ladder[l] = z * ladder[l - 1] * ((2 * l - 1) / (l - m)) - square * ladder[l - 2] * (
+                    (l + m - 1) / (l - m)
+                )
+            scale = y_factor(l, m) * double
+            part = ladder[l] * scale if l > m else scale
+            if m == 0:
+                emit(l * l, part if l > m else jnp.full_like(x, part))
+            else:
+                emit(l * l + 2 * m - 1, cos_m * part)
+                emit(l * l + 2 * m, sin_m * part)
+
+
+def split3(value):
+    high = value.astype(jnp.bfloat16).astype(jnp.float32)
+    rest = value - high
+    middle = rest.astype(jnp.bfloat16).astype(jnp.float32)
+    return high, middle, rest - middle
+
+
+FEATURES = 9
+FEATURE_ROWS = 6 * FEATURES + 3
+FAR_ROWS = 64
+
+
+def far_tables(atoms_ref, moments_ref, rows_ref, table_ref):
+    atoms = atoms_ref.shape[1]
+    ax = atoms_ref[0:1, :] - 8.0
+    ay = atoms_ref[1:2, :] - 8.0
+    az = atoms_ref[2:3, :] - 8.0
+    mom = [moments_ref[i : i + 1, :] for i in range(9)]
+    one, nil = jnp.ones_like(ax), jnp.zeros_like(ax)
+    n10, n11 = y_factor(1, 0), y_factor(1, 1)
+    vx, vy, vz = mom[2] * n11, mom[3] * n11, mom[1] * n10
+    f20, f21, f22 = y_factor(2, 0), 3.0 * y_factor(2, 1), 3.0 * y_factor(2, 2)
+    qzz = mom[4] * f20
+    qxx = mom[7] * f22 - qzz * 0.5
+    qyy = -mom[7] * f22 - qzz * 0.5
+    qxz, qyz, qxy = mom[5] * f21, mom[6] * f21, mom[8] * (2.0 * f22)
+    gx = -(2.0 * qxx * ax + qxy * ay + qxz * az)
+    gy = -(qxy * ax + 2.0 * qyy * ay + qyz * az)
+    gz = -(qxz * ax + qyz * ay + 2.0 * qzz * az)
+    const = -0.5 * (gx * ax + gy * ay + gz * az)
+    norm = ax * ax + ay * ay + az * az + 1.0
+    plans = [
+        ([-2.0 * ax, -2.0 * ay, -2.0 * az, one, one, one, nil, nil, nil], norm),
+        ([vx, vy, vz, nil, nil, nil, nil, nil, nil], -(vx * ax + vy * ay + vz * az)),
+        ([gx, gy, gz, qxx, qyy, qzz, qxy, qxz, qyz], const),
+    ]
+    for q, (coefs, fixed) in enumerate(plans):
+        columns = pl.ds(q * atoms, atoms)
+        for f, coef in enumerate(coefs):
+            high, middle, low = split3(coef)
+            for r, row in enumerate((high, middle, high, low, high, middle)):
+                rows_ref[6 * f + r : 6 * f + r + 1, columns] = row
+        for r, row in enumerate(split3(fixed)):
+            rows_ref[6 * FEATURES + r : 6 * FEATURES + r + 1, columns] = row
+        rows_ref[FEATURE_ROWS:FAR_ROWS, columns] = jnp.zeros(
+            (FAR_ROWS - FEATURE_ROWS, atoms), jnp.float32
+        )
+    table_ref[...] = rows_ref[...].astype(jnp.bfloat16)
+
+
+def point_features(px, py, pz, rows_ref):
+    qx, qy, qz = px - 8.0, py - 8.0, pz - 8.0
+    values = [qx, qy, qz, qx * qx, qy * qy, qz * qz, qx * qy, qx * qz, qy * qz]
+    for f, value in enumerate(values):
+        high, middle, low = split3(value)
+        for r, row in enumerate((high, high, middle, high, low, middle)):
+            rows_ref[6 * f + r : 6 * f + r + 1, :] = row
+    rows_ref[6 * FEATURES : FEATURE_ROWS, :] = jnp.ones((3, qx.shape[1]), jnp.float32)
+    rows_ref[FEATURE_ROWS:FAR_ROWS, :] = jnp.zeros(
+        (FAR_ROWS - FEATURE_ROWS, qx.shape[1]), jnp.float32
+    )
+    return rows_ref[...].T.astype(jnp.bfloat16)
+
+
+def evaluate_kernel(
+    near_smem,
+    near_ref,
+    points_ref,
+    slot_table_ref,
+    slot_pot_ref,
+    atoms_ref,
+    moments_ref,
+    centre_ref,
+    rate_ref,
+    out_ref,
+    far_rows,
+    far_table,
+    feat_rows,
+    far_acc,
+    y_rows,
+    rho_rows,
+    corr_ref,
+):
+    b = pl.program_id(0)
+    near_count = near_ref.shape[2]
+    pts = points_ref.shape[1]
+    atoms = atoms_ref.shape[1]
+
+    @pl.when(b == 0)
+    def _():
+        far_tables(atoms_ref, moments_ref, far_rows, far_table)
+        y_rows[...] = jnp.zeros_like(y_rows)
+
+    px, py, pz = points_ref[0:1, :], points_ref[1:2, :], points_ref[2:3, :]
+
+    features = point_features(px, py, pz, feat_rows)
+    far_acc[...] = jnp.zeros_like(far_acc)
+    chunk = 256
+
+    @pl.loop(0, atoms // chunk)
+    def _(c):
+        base = pl.multiple_of(c * chunk, chunk)
+
+        def table(q):
+            return far_table[:, pl.ds(pl.multiple_of(q * atoms + base, chunk), chunk)]
+
+        square = jnp.dot(features, table(0), preferred_element_type=jnp.float32)
+        linear = jnp.dot(features, table(1), preferred_element_type=jnp.float32)
+        quad = jnp.dot(features, table(2), preferred_element_type=jnp.float32)
+        inv = lax.rsqrt(square)
+        inv2 = inv * inv
+        level = moments_ref[0:1, pl.ds(base, chunk)] * y_factor(0, 0)
+        value = inv * (level + inv2 * (linear + inv2 * quad))
+        far_acc[...] += value[:, 0:128] + value[:, 128:256]
+
+    far_row = jnp.sum(far_acc[...].T, axis=0, keepdims=True)
+
+    hot = (
+        lax.broadcasted_iota(jnp.int32, (slot_table_ref.shape[0], near_count), 0) == near_ref[0]
+    ).astype(jnp.float32)
+    info = lax.dot_general(
+        hot,
+        slot_table_ref[...],
+        (((0,), (0,)), ((), ())),
+        precision=lax.Precision.HIGHEST,
+        preferred_element_type=jnp.float32,
+    )
+    step = 8
+    corr = jnp.zeros((step, pts), jnp.float32)
+    for j in range(0, near_count, step):
+        part = info[j : j + step, :]
+        dx = px - part[:, 0:1]
+        dy = py - part[:, 1:2]
+        dz = pz - part[:, 2:3]
+        square = dx * dx + dy * dy + dz * dz + 1.0
+        inv = lax.rsqrt(square)
+        rho_rows[j : j + step, :] = square * inv
+        low = {}
+
+        def emit(i, value):
+            y_rows[pl.ds(j * YR + i, step, stride=YR), :] = value
+            if i < 9:
+                low[i] = value
+
+        harmonic_rows(dx * inv, dy * inv, dz * inv, 6, emit)
+        term = [part[:, 3 + i : 4 + i] * low[i] for i in range(9)]
+        degree1 = term[1] + term[2] + term[3]
+        degree2 = (term[4] + term[5]) + (term[6] + term[7]) + term[8]
+        corr = corr + inv * (term[0] + inv * (degree1 + inv * degree2))
+    corr_ref[...] = corr
+
+    centre, rate = centre_ref[...], rate_ref[...]
+    unroll = 4
+
+    def pairs(g, total):
+        for v in range(unroll):
+            j = g * unroll + v
+            coefs = slot_pot_ref[near_smem[b, j]]
+            t = (rho_rows[pl.ds(j, 1), :] - centre) * rate
+            radial = jnp.exp2(-(t * t)).astype(jnp.bfloat16)
+            values = jnp.dot(coefs, radial, preferred_element_type=jnp.float32)
+            rows = y_rows[pl.ds(pl.multiple_of(j * YR, YR), YR), :]
+            total = total + values[0:YR] * rows
+        return total
+
+    total = lax.fori_loop(
+        0, near_count // unroll, pairs, jnp.zeros((YR, pts), jnp.float32)
+    )
+    near_row = jnp.sum(total, axis=0, keepdims=True)
+    out_ref[0] = near_row + far_row - jnp.sum(corr_ref[...], axis=0, keepdims=True)
+
+
+def evaluate(points, near_slot, slot_table, slot_pot, atom_pos, moments, decay_rates):
+    batches, near_count = near_slot.shape
+    pts = points.shape[1] // batches
+    atoms = atom_pos.shape[1]
     centres, spacing = shell_layout(decay_rates)
-    radial = shell_values(
-        distance[:, :, None, :],
-        decay_rates[None, None, :, None],
-        centres[None, None, :, None],
-        spacing,
-    ).astype(jnp.bfloat16)
-    values = jnp.einsum("bjik,bjkp->bjip", near_coef, radial, preferred_element_type=jnp.float32)
-    return jnp.sum(values * jnp.moveaxis(harmonics, 0, 2), axis=(1, 2)).reshape(-1)
-
-
-def far_field(points, near_ids, moments, atom_pos):
-    batches = near_ids.shape[0]
-    batch_pts = points.shape[1] // batches
-    grouped = jnp.moveaxis(points.reshape(3, batches, batch_pts), 1, 0)
-    atom_index = jnp.arange(atom_pos.shape[1])
-
-    def one_batch(inputs):
-        coords, ids = inputs
-        delta = coords[:, :, None] - atom_pos[:, None, :]
-        distance, unit_vec = soft_geometry(delta)
-        harmonics = harmonic_table(unit_vec[0], unit_vec[1], unit_vec[2], 2)
-        inverse = 1.0 / distance
-        keep = 1.0 - jnp.sum((ids[:, None] == atom_index[None, :]).astype(jnp.float32), axis=0)
-        scaled = moments * keep[None, :]
-        total = harmonics[0] * scaled[0][None, :] * inverse
-        total = total + jnp.sum(harmonics[1:4] * scaled[1:4, None, :], axis=0) * inverse * inverse
-        total = (
-            total
-            + jnp.sum(harmonics[4:9] * scaled[4:9, None, :], axis=0) * inverse * inverse * inverse
-        )
-        return jnp.sum(total, axis=1)
-
-    return lax.map(one_batch, (grouped, near_ids)).reshape(-1)
+    rate = jnp.sqrt(decay_rates * math.log2(math.e)) / spacing
+    centre_full = jnp.broadcast_to(centres[:, None], (NRAD, pts))
+    rate_full = jnp.broadcast_to(rate[:, None], (NRAD, pts))
+
+    def whole(shape):
+        return pl.BlockSpec(shape, lambda b, near: (0,) * len(shape))
+
+    out = pl.pallas_call(
+        evaluate_kernel,
+        out_shape=jax.ShapeDtypeStruct((batches, 1, pts), jnp.float32),
+        grid_spec=pltpu.PrefetchScalarGridSpec(
+            num_scalar_prefetch=1,
+            grid=(batches,),
+            in_specs=[
+                pl.BlockSpec((1, 1, near_count), lambda b, near: (b, 0, 0)),
+                pl.BlockSpec((3, pts), lambda b, near: (0, b)),
+                whole(slot_table.shape),
+                whole(slot_pot.shape),
+                whole(atom_pos.shape),
+                whole(moments.shape),
+                whole((NRAD, pts)),
+                whole((NRAD, pts)),
+            ],
+            out_specs=pl.BlockSpec((1, 1, pts), lambda b, near: (b, 0, 0)),
+            scratch_shapes=[
+                pltpu.VMEM((FAR_ROWS, 3 * atoms), jnp.float32),
+                pltpu.VMEM((FAR_ROWS, 3 * atoms), jnp.bfloat16),
+                pltpu.VMEM((FAR_ROWS, pts), jnp.float32),
+                pltpu.VMEM((pts, 128), jnp.float32),
+                pltpu.VMEM((near_count * YR, pts), jnp.float32),
+                pltpu.VMEM((near_count, pts), jnp.float32),
+                pltpu.VMEM((8, pts), jnp.float32),
+            ],
+        ),
+        compiler_params=pltpu.CompilerParams(
+            dimension_semantics=("arbitrary",), vmem_limit_bytes=40 << 20
+        ),
+        name="evaluate",
+    )(
+        near_slot,
+        near_slot.reshape(batches, 1, near_count),
+        points,
+        slot_table,
+        slot_pot,
+        atom_pos,
+        moments,
+        centre_full,
+        rate_full,
+    )
+    return out.reshape(-1)
 
 
 def per_device(
@@ -229,22 +456,12 @@
     column = owner * OWN + atom_index - starts[owner]
     moments_all = gathered[:, column]
     slot_pot = jnp.dot(packing.T, returned, preferred_element_type=jnp.float32).astype(jnp.bfloat16)
-    near_ids = my_list[near_slot]
-    group_ids = near_ids.reshape(groups, block, near_count)
-    list_index = jnp.arange(listed)
-
-    def near_group(inputs):
-        points, ids, near_list = inputs
-        picker = (near_list[:, :, None] == list_index[None, None, :]).astype(jnp.bfloat16)
-        near_coef = jnp.einsum(
-            "bjt,tw->bjw", picker, slot_pot, preferred_element_type=jnp.float32
-        ).astype(jnp.bfloat16)
-        near_coef = near_coef.reshape(block, near_count, HARM, NRAD)
-        return near_field(points, ids, near_coef, atom_pos, decay_rates)
-
-    near_part = lax.map(near_group, (group_points, group_ids, group_near)).reshape(-1)
-    far_part = far_field(grid_points, near_ids, moments_all, atom_pos)
-    return near_part + far_part
+    padded = jnp.pad(slot_pot.reshape(listed, HARM, NRAD), ((0, 0), (0, HP - HARM), (0, 0)))
+    slot_table = jnp.concatenate([atom_pos[:, my_list], moments_all[:, my_list]], axis=0).T
+    slot_table = jnp.pad(slot_table, ((0, 0), (0, 128 - slot_table.shape[1])))
+    return evaluate(
+        grid_points, near_slot, slot_table, padded, atom_pos, moments_all, decay_rates
+    )
 
 
 def solution(mesh):

time: 604 us -> 498 us (0.82)
  other arithmetic: 124 us -> 28.6 us
  Pallas kernels: 0 us -> 87.7 us
  matrix products: 70.1 us -> 29.2 us
  local copies, waits for them, and re-layouts: 286 us -> 249 us
  blocking collectives: 93.8 us -> 78.4 us
    pallas_call x0 -> x1, Pallas kernels: none -> 87.7 us  [evaluate(): pl.pallas_call(evaluate_kernel, out_shape=jax.ShapeDtypeStruct((batches,...]
    reduce_sum x68 -> x0, other arithmetic: 43.5 us -> none  [the longest x4 17.1 us: near_field(): jnp.sum(values * jnp.moveaxis(harmonics, 0, 2), axis=(1, 2)).reshape(-1)]
    dot_general x8 -> x0, matrix products: 31.9 us -> none  [the longest x4 27.8 us: near_field(): jnp.einsum('bjik,bjkp->bjip', near_coef, radial, preferred_element_type=j...]
    while x236 -> x0, other arithmetic: 21 us -> none
    while x44 -> x24, local copies, waits for them, and re-layouts: 15.4 us -> 0.05 us
    all_gather x1, blocking collectives: 93.8 us -> 78.4 us  [per_device(): gathered = lax.all_gather(moments_own, ('sx', 'sy'), axis=1, tiled=True)]
    gather x10 -> x2, local copies, waits for them, and re-layouts: 14.8 us -> 3.75 us  [the longest x1 1.88 us: per_device(): moments_all[:, my_list]]
    reshape x5 -> x1, local copies, waits for them, and re-layouts: 12.3 us -> 2.72 us  [per_device(): slot_pot.reshape(listed, HARM, NRAD)]
  transfers between devices with their start and end apart: 2 -> 2, of which waited for: 0 -> 0; matrix products, arithmetic and copies ran while one was open for 28% -> 19% of each run, Pallas kernels for 0% -> 0%
where the time goes in v1:
time: 498 us; the launch traced here: 495 us
  local copies, waits for them, and re-layouts  249 us (50%)
  Pallas kernels  87.7 us (18%)
  blocking collectives  78.4 us (16%)
  matrix products  29.2 us (6%)
  other arithmetic  28.6 us (6%)
  starting transfers between devices  21.2 us (4%)
    gather x2, local copies, waits for them, and re-layouts, per_device(): owners_all = owner[all_lists]  90.6 us
    pallas_call x1, Pallas kernels, evaluate(): pl.pallas_call(evaluate_kernel, out_shape=jax.ShapeDtypeStruct((batches,...  87.7 us
    all_gather x1, blocking collectives, per_device(): gathered = lax.all_gather(moments_own, ('sx', 'sy'), axis=1, tiled=True)  78.4 us
    scatter x1, local copies, waits for them, and re-layouts, per_device(): row_owned = jnp.full((devices * capacity + 1,), OWN, jnp.int32).at[target...  60.5 us
    dot_general x4, matrix products, project_points(): jnp.einsum('tip,kp->tik', weighted, radial, preferred_element_type=jnp.fl...  18.2 us
    all_to_all x3, local copies, waits for them, and re-layouts, per_device(): lax.all_to_all(outgoing, ('sx', 'sy'), split_axis=0, concat_axis=0, tiled...  14.4 us
    gather x4, local copies, waits for them, and re-layouts, project_points(): atom_ids = atom_list[slot_of_point]  13.4 us
    gather x1, local copies, waits for them, and re-layouts, per_device(): column = owner * OWN + atom_index - starts[owner]  12.6 us
  transfers between devices with their start and end apart: 2, of which 0 were waited for; matrix products, arithmetic and copies ran while one was open for 19% of the time, Pallas kernels for 0%

profile of v1, /device:TPU:1, one launch (start us, length us, event | category | flops | bytes accessed | tf_op | source)
XLA Modules:
  0.0 495.3 jit_solution(3911288104610266616)
XLA Ops:
  0.7 0.9 fusion.27
  1.6 90.5 %gather_fusion.3 = s32[16384]{0:T(1024)S(1)} fusion(s32[2048]{0:T(1024)S(1)} %convert_reduce_fusion, s32[16384]{0:T(1024)S(1)} %fusion.27), kind=kCustom, calls=%fused_computation.3 | custom fusion | bytes 196608 | tf_op jit(solution)/shard_map/gather | solution.py:425
  92.3 1.3 copy.265
  94.9 1.2 fusion.56
  96.1 79.3 %while.16 = (s32[]{:T(128)}, f32[128,6272]{0,1:T(8,128)S(1)}, s32[4,512]{1,0:T(4,128)S(1)}, f32[4,512]{1,0:T(4,128)}, f32[4,3,512]{2,1,0:T(4,128)}, /*index=5*/s...) while((s32[]{:T(128)}, f32[128,6272]{0,1:T(8,128)S(1)}, ...), condition=%wide.region_7.8_spmd.clone, body=%wide.region_5.7_spmd.clone.sunk | while | flops 827510272 | bytes 13908703 | solution.py:409
  96.2 3.3 gather_fusion
  99.5 2.3 gather_fusion.1
  101.9 0.7 multiply_reduce_fusion.2
  102.7 0.7 broadcast_divide_fusion.2
  104.3 2.9 stack.9
  107.2 0.7 constant_dynamic-slice_fusion.6
  108.0 0.7 multiply_bitcast_fusion.2
  108.6 4.6 fusion.92
  113.2 2.7 bitcast_add_fusion.3
  116.0 3.3 gather_fusion
  119.4 2.3 gather_fusion.1
  121.8 0.7 multiply_reduce_fusion.2
  122.5 0.7 broadcast_divide_fusion.2
  124.1 2.9 stack.9
  127.0 0.7 constant_dynamic-slice_fusion.6
  127.8 0.7 multiply_bitcast_fusion.2
  128.5 4.5 fusion.92
  133.0 2.7 bitcast_add_fusion.3
  135.8 3.3 gather_fusion
  139.2 2.3 gather_fusion.1
  141.6 0.7 multiply_reduce_fusion.2
  142.4 0.7 broadcast_divide_fusion.2
  143.9 2.9 stack.9
  146.9 0.7 constant_dynamic-slice_fusion.6
  148.3 4.5 fusion.92
  152.9 2.7 bitcast_add_fusion.3
  155.7 3.3 gather_fusion
  159.1 2.3 gather_fusion.1
  161.4 0.7 multiply_reduce_fusion.2
  162.2 0.7 broadcast_divide_fusion.2
  163.8 2.9 stack.9
  166.7 0.7 constant_dynamic-slice_fusion.6
  168.1 4.5 fusion.92
  172.7 2.7 bitcast_add_fusion.3
  175.5 3.3 convolution_convert_fusion.1
  178.8 7.1 %all_to_all.16 = bf16[128,2,6272]{2,1,0:T(2,128)(2,1)} reshape(bf16[256,6272]{1,0:T(8,128)(2,1)} %convolution_convert_fusion.1) | data formatting | bytes 6422528 | tf_op jit(solution)/shard_map/all_to_all | solution.py:446
  185.9 11.5 %all-to-all-start = ((bf16[128,2,6272]{2,1,0:T(2,128)(2,1)}), bf16[128,2,6272]{2,1,0:T(2,128)(2,1)S(1)}, u32[]{:S(2)}, u32[]{:S(2)}) async-start(bf16[128,2,6272]{2,1,0:T(2,128)(2,1)} %all_to_all.16), calls=%async_computation | async-start | bytes 6422528 | tf_op jit(solution)/shard_map/all_to_all | solution.py:446
  199.0 0.7 add_select_fusion
  200.5 60.5 %scatter_custom_fusion = s32[257]{0:T(512)S(1)} fusion(s32[16384]{0:T(1024)S(1)} %bitcast.187, s32[16384]{0:T(1024)S(1)} %subtract_select_fusion, s32[]{:T(128)} %constant.501.clone.1), kind=kCustom, calls=%fused_computation.180 | custom fusion | bytes 1032 | tf_op jit(solution)/shard_map/scatter | solution.py:444
  261.0 2.7 all_to_all.18
  263.7 4.5 copy.270
  268.3 1.0 fusion.46
  271.2 1.0 convolution_convert_fusion
  272.3 2.7 all_to_all.19
  275.0 9.7 %all-to-all-start.1 = ((bf16[128,2,6272]{2,1,0:T(2,128)(2,1)}), bf16[128,2,6272]{2,1,0:T(2,128)(2,1)S(1)}, u32[]{:S(2)}, u32[]{:S(2)}) async-start(bf16[128,2,6272]{2,1,0:T(2,128)(2,1)} %all_to_all.19), calls=%async_computation.1 | async-start | bytes 6422528 | tf_op jit(solution)/shard_map/all_to_all | solution.py:454
  284.8 12.6 %gather_fusion.5 = s32[2048]{0:T(1024)S(1)} fusion(s32[128]{0:T(128)S(1)} %fusion.54, s32[2048]{0:T(1024)S(1)} %broadcast_clamp_fusion.1), kind=kCustom, calls=%fused_computation.5 | custom fusion | bytes 24576 | tf_op jit(solution)/shard_map/gather | solution.py:456
  297.5 1.9 gather_fusion.2
  300.0 1.2 fusion.50
  301.2 78.4 %all-gather = f32[128,32,9]{1,2,0:T(8,128)} all-gather(f32[1,32,9]{1,2,0:T(8,128)S(1)} %bitcast.188), channel_id=1, replica_groups=mesh['sx'=8,'sy'=16] {'sx','sy'}, dimensions={0}, use_global_device_ids=true | all-gather | bytes 148608 | tf_op jit(solution)/shard_map/all_gather | solution.py:455
  379.6 3.4 copy.271
  383.0 9.2 %gather_fusion.6 = f32[2048,9]{1,0:T(8,128)} fusion(f32[9,4096]{0,1:T(8,128)} %bitcast.170, s32[2048]{0:T(1024)S(1)} %broadcast_clamp_fusion), kind=kCustom, calls=%fused_computation.6 | custom fusion | bytes 155648 | tf_op jit(solution)/shard_map/gather | solution.py:457
  392.3 1.5 copy.272
  393.8 1.9 gather_fusion.7
  395.8 2.7 all_to_all.21
  398.6 2.5 convolution_convert_fusion.2
  401.1 1.7 copy.275
  402.9 2.7 copy.276
  405.6 1.8 pad.9.slot_pot_ref
  407.6 87.7 %evaluate.1 = f32[16,1,128]{2,1,0:T(1,128)} custom-call(s32[16,64]{1,0:T(8,128)S(1)} %copy-done.2, s32[16,1,64]{2,1,0:T(1,128)S(1)} %bitcast.165, f32[3,2048]{1,0:T(4,128)S(1)} %bitcast.173, f32[128,128]{1,0:T(8,128)S(1)} %pad.8.slot_table_ref, bf16[128,64,128]{2,1,0:T(8,128)(2,1)S(1)} %pad.9.slot_pot_ref, f32[3,2048]{1,0:T(4,128)S(1)} %copy-done.1, ...), custom_call_target="tpu_custom_call" | custom-call | tf_op jit(solution)/shard_map/evaluate/pallas_call | solution.py:326
  (183 shorter events, 12.4 us)
Async XLA Ops:
  0.0 299.4 %copy-start = (f32[3,128]{1,0:T(4,128)S(1)}, f32[3,128]{1,0:T(4,128)}, u32[]{:S(2)}) copy-start(f32[3,128]{1,0:T(4,128)} %param.21) | copy-start | bytes 4612
  0.3 1.2 copy-start.15
  1.5 90.8 %copy-start.1 = (f32[3,2048]{1,0:T(4,128)S(1)}, f32[3,2048]{1,0:T(4,128)}, u32[]{:S(2)}) copy-start(f32[3,2048]{1,0:T(4,128)} %atoms_ref.1) | copy-start | bytes 73732
  1.6 92.1 %copy-start.19 = (f32[128]{0:T(128)S(1)}, f32[128]{0:T(128)}, u32[]{:S(2)}) copy-start(f32[128]{0:T(128)} %param.19) | copy-start | bytes 1540
  1.6 92.7 %copy-start.12 = (s32[2048]{0:T(1024)S(1)}, s32[2048]{0:T(1024)}, u32[]{:S(2)}) copy-start(s32[2048]{0:T(1024)} %param.15) | copy-start | bytes 24580
  1.6 92.7 %copy-start.13 = (f32[2048]{0:T(1024)S(1)}, f32[2048]{0:T(1024)}, u32[]{:S(2)}) copy-start(f32[2048]{0:T(1024)} %param.14) | copy-start | bytes 24580
  92.1 4.0 copy-start.7
  96.1 3.4 copy-start.10
  102.7 1.4 copy-start.9
  113.2 2.8 copy-start.11
  116.0 3.4 copy-start.10
  122.5 1.4 copy-start.9
  133.0 2.8 copy-start.11
  135.8 3.4 copy-start.10
  142.3 1.4 copy-start.9
  152.9 2.8 copy-start.11
  155.6 3.4 copy-start.10
  162.2 1.4 copy-start.9
  172.7 2.8 copy-start.11
  185.9 11.5 %copy-start.16 = (s32[128]{0:T(128)S(1)}, s32[128]{0:T(128)}, u32[]{:S(2)}) copy-start(s32[128]{0:T(128)} %copy-done.15) | copy-start | bytes 1540
  185.9 11.5 %copy-start.8 = (s32[16384]{0:T(1024)S(1)}, s32[16384]{0:T(1024)}, u32[]{:S(2)}) copy-start(s32[16384]{0:T(1024)} %copy-done.7) | copy-start | bytes 196612
  185.9 13.8 %copy-start.6 = (s32[16384]{0:T(1024)S(1)}, s32[16384]{0:T(1024)}, u32[]{:S(2)}) copy-start(s32[16384]{0:T(1024)} %param.17) | copy-start | bytes 196612
  185.9 75.1 %all-to-all-start = ((bf16[128,2,6272]{2,1,0:T(2,128)(2,1)}), bf16[128,2,6272]{2,1,0:T(2,128)(2,1)S(1)}, u32[]{:S(2)}, u32[]{:S(2)}) async-start(bf16[128,2,6272]{2,1,0:T(2,128)(2,1)} %all_to_all.16), calls=%async_computation | async-start | bytes 6422528 | tf_op jit(solution)/shard_map/all_to_all | solution.py:446
  268.3 1.1 copy-start.4
  269.3 1.5 copy-start.3
  275.0 120.8 %all-to-all-start.1 = ((bf16[128,2,6272]{2,1,0:T(2,128)(2,1)}), bf16[128,2,6272]{2,1,0:T(2,128)(2,1)S(1)}, u32[]{:S(2)}, u32[]{:S(2)}) async-start(bf16[128,2,6272]{2,1,0:T(2,128)(2,1)} %all_to_all.19), calls=%async_computation.1 | async-start | bytes 6422528 | tf_op jit(solution)/shard_map/all_to_all | solution.py:454
  284.8 12.7 %copy-start.18 = (s32[9]{0:T(128)S(1)}, s32[9]{0:T(128)}, u32[]{:S(2)}) copy-start(s32[9]{0:T(128)} %constant.524) | copy-start | bytes 112
  395.8 2.8 copy-start.14
  402.8 4.6 copy-start.17
  402.8 4.8 copy-start.2
  402.9 4.8 copy-start.5

commit v2 on v1

--- a/solution.py
+++ b/solution.py
@@ -1,8 +1,8 @@
+import functools
 import math
 
 import jax
 import jax.numpy as jnp
-import numpy as np
 from jax import lax
 from jax.experimental import pallas as pl
 from jax.experimental.pallas import tpu as pltpu
@@ -10,45 +10,6 @@
 
 HARM = 49
 NRAD = 128
-OWN_AVG = 16
-OWN = 32
-
-
-def harmonic_table(comp_x, comp_y, comp_z, top_degree):
-    square = comp_x * comp_x + comp_y * comp_y + comp_z * comp_z
-    cosines = [jnp.ones_like(comp_x)]
-    sine_terms = [jnp.zeros_like(comp_x)]
-    for m in range(1, top_degree + 1):
-        cosines.append(cosines[m - 1] * comp_x - sine_terms[m - 1] * comp_y)
-        sine_terms.append(cosines[m - 1] * comp_y + sine_terms[m - 1] * comp_x)
-    legendre = {}
-    for m in range(top_degree + 1):
-        legendre[m, m] = float(math.prod(range(1, 2 * m, 2))) * cosines[0]
-        if m + 1 <= top_degree:
-            legendre[m + 1, m] = (2 * m + 1) * comp_z * legendre[m, m]
-        for l in range(m + 2, top_degree + 1):
-            legendre[l, m] = (
-                (2 * l - 1) * comp_z * legendre[l - 1, m]
-                - (l + m - 1) * square * legendre[l - 2, m]
-            ) / (l - m)
-    stacked = []
-    for l in range(top_degree + 1):
-        for m in range(l + 1):
-            factor = math.sqrt(
-                (2 * l + 1) / (4 * math.pi) * math.factorial(l - m) / math.factorial(l + m)
-            )
-            if m == 0:
-                stacked.append(factor * legendre[l, 0])
-            else:
-                factor = factor * math.sqrt(2.0)
-                stacked.append(factor * legendre[l, m] * cosines[m])
-                stacked.append(factor * legendre[l, m] * sine_terms[m])
-    return jnp.stack(stacked)
-
-
-def soft_geometry(delta):
-    distance = jnp.sqrt(jnp.sum(delta * delta, axis=0) + 1.0)
-    return (distance, delta / distance)
 
 
 def shell_layout(decay_rates):
@@ -56,48 +17,6 @@
     spacing = 27.0 / (count - 1)
     centres = 1.0 + spacing * jnp.arange(count).astype(decay_rates.dtype)
     return (centres, spacing)
-
-
-def shell_values(distance, rates, centres, spacing):
-    offset = (distance - centres) / spacing
-    return jnp.exp(-rates * offset * offset)
-
-
-def project_points(points, density, slot_of_point, atom_list, atom_pos, decay_rates):
-    listed = atom_list.shape[0]
-    atom_ids = atom_list[slot_of_point]
-    delta = points - atom_pos[:, atom_ids]
-    distance, unit_vec = soft_geometry(delta)
-    harmonics = harmonic_table(unit_vec[0], unit_vec[1], unit_vec[2], 6)
-    projected = (density[None, :] * harmonics).astype(jnp.bfloat16)
-    centres, spacing = shell_layout(decay_rates)
-    radial = shell_values(
-        distance[None, :], decay_rates[:, None], centres[:, None], spacing
-    ).astype(jnp.bfloat16)
-    onehot = (slot_of_point[None, :] == jnp.arange(listed)[:, None]).astype(jnp.bfloat16)
-    weighted = onehot[:, None, :] * projected[None, :, :]
-    terms = jnp.einsum("tip,kp->tik", weighted, radial, preferred_element_type=jnp.float32)
-    return terms.reshape(listed, -1)
-
-
-def apply_green(coefficients, green):
-    pieces = []
-    for l in range(7):
-        pieces.append(
-            jnp.einsum(
-                "aik,kn->ain",
-                coefficients[:, l * l : (l + 1) * (l + 1)],
-                green[l],
-                precision=lax.Precision.HIGHEST,
-            )
-        )
-    return jnp.concatenate(pieces, axis=1)
-
-
-def low_moments(coefficients, moment_table):
-    degrees = np.array([0, 1, 1, 1, 2, 2, 2, 2, 2])
-    table = moment_table[degrees]
-    return jnp.einsum("aik,ik->ia", coefficients[:, :9], table, precision=lax.Precision.HIGHEST)
 
 
 HP = 64
@@ -368,6 +287,462 @@
     return out.reshape(-1)
 
 
+def point_blocks_kernel(
+    points_ref,
+    density_ref,
+    slots_ref,
+    places_ref,
+    centre_ref,
+    rate_ref,
+    table_ref,
+    out_ref,
+    four_ref,
+    q_rows,
+):
+    listed = places_ref.shape[1]
+    pts = centre_ref.shape[1]
+    blocks = points_ref.shape[1] // pts
+    slot_rows = lax.broadcasted_iota(jnp.int32, (listed, pts), 0)
+    lane = lax.broadcasted_iota(jnp.int32, (listed, pts), 1)
+    earlier = (slot_rows < lane).astype(jnp.bfloat16)
+    counts = jnp.zeros((listed, 1), jnp.float32)
+    ranks, hots = [], []
+    for g in range(blocks):
+        at = pl.ds(g * pts, pts)
+        same = slot_rows == slots_ref[:, at]
+        hot = same.astype(jnp.float32)
+        inside = jnp.dot(hot.astype(jnp.bfloat16), earlier, preferred_element_type=jnp.float32)
+        ranks.append(jnp.sum(hot * (inside + counts), axis=0, keepdims=True))
+        counts = counts + jnp.sum(hot, axis=1, keepdims=True)
+    below = (lax.broadcasted_iota(jnp.int32, (listed, listed), 1) < lax.broadcasted_iota(
+        jnp.int32, (listed, listed), 0
+    )).astype(jnp.float32)
+    counts_full = jnp.broadcast_to(counts, (listed, listed))
+    starts_full = jnp.dot(
+        below, counts_full, precision=lax.Precision.HIGHEST, preferred_element_type=jnp.float32
+    )
+    starts = starts_full[:, 0:1]
+    packed = starts_full * 4096.0 + counts_full
+    rows64 = lax.broadcasted_iota(jnp.int32, (4 * blocks, pts), 0) // 4
+    sorted_rows = jnp.zeros((4 * blocks, pts), jnp.float32)
+    moments = jnp.zeros((16, listed), jnp.float32)
+    q_rows[...] = jnp.zeros_like(q_rows)
+    for g in range(blocks):
+        at = pl.ds(g * pts, pts)
+        hot = (slot_rows == slots_ref[:, at]).astype(jnp.float32)
+        place = ranks[g] + jnp.sum(hot * starts, axis=0, keepdims=True)
+        place = place.astype(jnp.int32)
+        atom = jnp.dot(
+            places_ref[...], hot, precision=lax.Precision.HIGHEST, preferred_element_type=jnp.float32
+        )
+        dx = points_ref[0:1, at] - atom[0:1]
+        dy = points_ref[1:2, at] - atom[1:2]
+        dz = points_ref[2:3, at] - atom[2:3]
+        weight = density_ref[:, at]
+        for r in range(2):
+            for c, value in enumerate((dx, dy, dz, weight)):
+                four_ref[4 * r + c : 4 * r + c + 1, :] = value
+        tiled = jnp.concatenate([four_ref[...]] * (blocks // 2), axis=0)
+        masked = jnp.where(rows64 == place // pts, tiled, 0.0)
+        target = (slot_rows == place % pts).astype(jnp.bfloat16)
+        for piece in split3(masked):
+            sorted_rows = sorted_rows + lax.dot_general(
+                piece.astype(jnp.bfloat16),
+                target,
+                (((1,), (1,)), ((), ())),
+                preferred_element_type=jnp.float32,
+            )
+        square = dx * dx + dy * dy + dz * dz + 1.0
+        inv = lax.rsqrt(square)
+        rho = square * inv
+        t = (rho - centre_ref[...]) * rate_ref[...]
+        radial = jnp.exp2(-(t * t))
+        levels = jnp.dot(
+            table_ref[...], radial, precision=lax.Precision.HIGHEST, preferred_element_type=jnp.float32
+        )
+
+        def emit(i, value):
+            degree = (0, 1, 1, 1, 2, 2, 2, 2, 2)[i]
+            q_rows[i : i + 1, :] = value * weight * levels[degree : degree + 1]
+
+        harmonic_rows(dx * inv, dy * inv, dz * inv, 2, emit)
+        moments = moments + lax.dot_general(
+            q_rows[...],
+            hot,
+            (((1,), (1,)), ((), ())),
+            precision=lax.Precision.HIGHEST,
+            preferred_element_type=jnp.float32,
+        )
+    out_ref[0 : 4 * blocks, :] = sorted_rows
+    out_ref[4 * blocks : 4 * blocks + 1, :] = packed.T[0:1, :]
+    out_ref[4 * blocks + 1 : 4 * blocks + 10, :] = moments[0:9]
+    out_ref[4 * blocks + 10 : 4 * blocks + 12, :] = jnp.zeros((2, listed), jnp.float32)
+
+
+def radial_tables(decay_rates, width):
+    centres, spacing = shell_layout(decay_rates)
+    rate = jnp.sqrt(decay_rates * math.log2(math.e)) / spacing
+    shape = (decay_rates.shape[0], width)
+    return jnp.broadcast_to(centres[:, None], shape), jnp.broadcast_to(rate[:, None], shape)
+
+
+def point_blocks(points, density, slots, places, tables, moment_table):
+    count = points.shape[1]
+    pts = tables[0].shape[1]
+    rows = 4 * (count // pts) + 12
+    out = pl.pallas_call(
+        point_blocks_kernel,
+        out_shape=jax.ShapeDtypeStruct((rows, pts), jnp.float32),
+        scratch_shapes=[pltpu.VMEM((8, pts), jnp.float32), pltpu.VMEM((16, pts), jnp.float32)],
+        compiler_params=pltpu.CompilerParams(vmem_limit_bytes=40 << 20),
+        name="point_blocks",
+    )(
+        points,
+        density.reshape(1, count),
+        slots.reshape(1, count),
+        jnp.pad(places, ((0, 5), (0, 0))),
+        *tables,
+        jnp.pad(moment_table, ((0, 5), (0, 0))),
+    )
+    return out.reshape(rows // 4, 4, pts)
+
+
+MESH = pl.DeviceIdType.MESH
+SIDE = 4
+
+
+def gather_kernel(cuts, mine_ref, all_ref, local_sem, send_sems, recv_sems, swap_send, swap_recv):
+    row, column = lax.axis_index("sx"), lax.axis_index("sy")
+    core = lax.rem(row, 2)
+    here = {"z": row // 2, "y": column // SIDE, "x": lax.rem(column, SIDE)}
+
+    def device(place, on_core):
+        return (place["z"] * 2 + on_core, place["y"] * SIDE + place["x"])
+
+    def moved(axis, offset):
+        place = dict(here)
+        place[axis] = lax.rem(here[axis] + offset, SIDE)
+        return place
+
+    def region(place, whole, part):
+        index = [pl.ds(0, SIDE) if a in whole else place[a] for a in ("z", "y", "x")]
+        return all_ref.at[index[0], core, index[1], index[2], part]
+
+    barrier = pltpu.get_barrier_semaphore()
+    for axis in ("z", "y", "x"):
+        for offset in range(1, SIDE):
+            pl.semaphore_signal(
+                barrier, inc=1, device_id=device(moved(axis, offset), core), device_id_type=MESH
+            )
+    pl.semaphore_signal(barrier, inc=1, device_id=device(here, 1 - core), device_id_type=MESH)
+    pl.semaphore_wait(barrier, 3 * (SIDE - 1) + 1)
+
+    local = pltpu.make_async_copy(mine_ref, region(here, "", pl.ds(0, cuts[-1])), local_sem)
+    local.start()
+    orders = ("xyz", "yzx", "zxy")
+    parts = [pl.ds(cuts[c], cuts[c + 1] - cuts[c]) for c in range(3)]
+    hops = {}
+    swaps = []
+
+    def send(c, phase):
+        axis = orders[c][phase]
+        whole = orders[c][:phase]
+        for offset in range(1, SIDE):
+            place = region(here, whole, parts[c])
+            copy = pltpu.make_async_remote_copy(
+                src_ref=mine_ref.at[parts[c]] if phase == 0 else place,
+                dst_ref=place,
+                send_sem=send_sems.at[c, phase, offset],
+                recv_sem=recv_sems.at[c, phase, offset],
+                device_id=device(moved(axis, offset), core),
+                device_id_type=MESH,
+            )
+            copy.start()
+            hops[c, phase, offset] = copy
+
+    def swap(c, slot, place):
+        area = region(place, orders[c][:2], parts[c])
+        copy = pltpu.make_async_remote_copy(
+            src_ref=area,
+            dst_ref=area,
+            send_sem=swap_send.at[c, slot],
+            recv_sem=swap_recv.at[c, slot],
+            device_id=device(here, 1 - core),
+            device_id_type=MESH,
+        )
+        copy.start()
+        swaps.append(copy)
+
+    for c in range(3):
+        send(c, 0)
+    local.wait()
+    for phase in (1, 2):
+        for c in range(3):
+            for offset in range(1, SIDE):
+                hops[c, phase - 1, offset].wait_recv()
+            send(c, phase)
+    for c in range(3):
+        swap(c, 0, here)
+    for offset in range(1, SIDE):
+        for c in range(3):
+            hops[c, 2, offset].wait_recv()
+            swap(c, offset, moved(orders[c][2], SIDE - offset))
+    for copy in hops.values():
+        copy.wait_send()
+    for copy in swaps:
+        copy.wait()
+
+
+def gather_blocks(mine):
+    blocks = mine.shape[0]
+    cuts = (0, blocks // 3, 2 * blocks // 3, blocks)
+    return pl.pallas_call(
+        functools.partial(gather_kernel, cuts),
+        out_shape=jax.ShapeDtypeStruct((SIDE, 2, SIDE, SIDE) + mine.shape, mine.dtype),
+        in_specs=[pl.BlockSpec(memory_space=pl.ANY)],
+        out_specs=pl.BlockSpec(memory_space=pl.ANY),
+        scratch_shapes=[
+            pltpu.SemaphoreType.DMA,
+            pltpu.SemaphoreType.DMA((3, 3, SIDE)),
+            pltpu.SemaphoreType.DMA((3, 3, SIDE)),
+            pltpu.SemaphoreType.DMA((3, SIDE)),
+            pltpu.SemaphoreType.DMA((3, SIDE)),
+        ],
+        compiler_params=pltpu.CompilerParams(collective_id=0, has_side_effects=True),
+        name="gather_blocks",
+    )(mine)
+
+
+CHUNK = 32
+PER = 4
+FLUSH = 8
+
+
+def project_kernel(
+    counts_ref,
+    codes_ref,
+    runs_ref,
+    blocks_ref,
+    centre_ref,
+    rate_ref,
+    green_ref,
+    pot_ref,
+    buffer,
+    owner_ref,
+    used_ref,
+    y_rows,
+    rho_rows,
+    coefs_ref,
+):
+    listed = counts_ref.shape[0]
+    pts = centre_ref.shape[1]
+    coefs_ref[...] = jnp.zeros_like(coefs_ref)
+    y_rows[...] = jnp.zeros_like(y_rows)
+    lane = lax.broadcasted_iota(jnp.int32, (4, pts), 1)
+    used_ref[0] = 0
+    for f in range(FLUSH):
+        owner_ref[f] = 0
+
+    def flush():
+        def component(c):
+            return buffer[pl.ds(c, FLUSH, stride=4), :]
+
+        dx, dy, dz, weight = (component(c) for c in range(4))
+        square = dx * dx + dy * dy + dz * dz + 1.0
+        inv = lax.rsqrt(square)
+        rho_rows[...] = square * inv
+
+        def emit(i, value):
+            y_rows[pl.ds(i, FLUSH, stride=HP), :] = value * weight
+
+        harmonic_rows(dx * inv, dy * inv, dz * inv, 6, emit)
+        sums = []
+        for f in range(FLUSH):
+            t = (rho_rows[f : f + 1, :] - centre_ref[...]) * rate_ref[...]
+            radial = jnp.exp2(-(t * t)).astype(jnp.bfloat16)
+            rows = y_rows[f * HP : (f + 1) * HP, :].astype(jnp.bfloat16)
+            sums.append(
+                lax.dot_general(
+                    rows, radial, (((1,), (1,)), ((), ())), preferred_element_type=jnp.float32
+                )
+            )
+        for f in range(FLUSH):
+            at = pl.ds(owner_ref[f], YR, stride=listed)
+            coefs_ref[at, :] = coefs_ref[at, :] + sums[f][0:YR]
+        buffer[...] = jnp.zeros_like(buffer)
+        used_ref[0] = 0
+
+    buffer[...] = jnp.zeros_like(buffer)
+
+    def window(device, start):
+        at = lax.shift_right_logical(start, 7)
+        off = lax.bitwise_and(start, 127)
+        first = blocks_ref[device, at]
+        second = blocks_ref[device, at + 1]
+        return jnp.where(lane >= off, first, second), off
+
+    def piece(device, start, length, position):
+        value, off = window(device, start)
+        left = position * CHUNK
+        moved = pltpu.roll(value, lax.bitwise_and(left - off + 128, 127), 1)
+        keep = (lane >= left) & (lane < left + length)
+        return jnp.where(keep, moved, 0.0)
+
+    def put(j, value):
+        row = used_ref[0]
+        buffer[pl.ds(row * 4, 4), :] = value
+        owner_ref[row] = j
+        used_ref[0] = row + 1
+
+        @pl.when(row + 1 == FLUSH)
+        def _():
+            flush()
+
+    @pl.loop(0, listed)
+    def _(j):
+        count = counts_ref[j]
+
+        @pl.loop(0, lax.shift_right_logical(count + (PER - 1), 2))
+        def _(g):
+            total = jnp.zeros((4, pts), jnp.float32)
+            longest = jnp.int32(0)
+            entries = []
+            for v in range(PER):
+                r = g * PER + v
+                code = codes_ref[r, j]
+                device = lax.shift_right_logical(code, 7)
+                run = runs_ref[device, lax.bitwise_and(code, 127)]
+                length = jnp.where(r < count, lax.bitwise_and(run, 4095), 0)
+                start = lax.shift_right_logical(run, 12)
+                entries.append((device, start, length))
+                longest = jnp.maximum(longest, length)
+                total = total + piece(device, start, jnp.minimum(length, CHUNK), v)
+            put(j, total)
+
+            @pl.when(longest > CHUNK)
+            def _():
+                for device, start, length in entries:
+
+                    @pl.loop(1, (length + (CHUNK - 1)) // CHUNK)
+                    def _(c):
+                        put(
+                            j,
+                            piece(
+                                device,
+                                start + c * CHUNK,
+                                jnp.minimum(length - c * CHUNK, CHUNK),
+                                0,
+                            ),
+                        )
+
+    flush()
+    for l in range(7):
+        top = green_ref[l]
+        high = top.astype(jnp.bfloat16)
+        low = (top - high.astype(jnp.float32)).astype(jnp.bfloat16)
+        half = jnp.concatenate([high, low], axis=1)
+        table = jnp.concatenate([half, half], axis=0)
+        for i in range(l * l, (l + 1) * (l + 1)):
+            rows = coefs_ref[i * listed : (i + 1) * listed, :]
+            big = rows.astype(jnp.bfloat16)
+            small = (rows - big.astype(jnp.float32)).astype(jnp.bfloat16)
+            both = jnp.dot(
+                jnp.concatenate([big, small], axis=1), table, preferred_element_type=jnp.float32
+            )
+            coefs_ref[i * listed : (i + 1) * listed, :] = both[:, 0:128] + both[:, 128:256]
+
+    @pl.loop(0, listed)
+    def _(j):
+        rows = coefs_ref[pl.ds(j, YR, stride=listed), :]
+        pot_ref[j] = jnp.concatenate(
+            [rows, jnp.zeros((HP - YR, rows.shape[1]), jnp.float32)], axis=0
+        ).astype(jnp.bfloat16)
+
+
+def project(counts, codes, runs, blocks, tables, green):
+    listed = counts.shape[0]
+    pts = tables[0].shape[1]
+    smem = pl.BlockSpec(memory_space=pltpu.SMEM)
+    vmem = pl.BlockSpec(memory_space=pltpu.VMEM)
+    return pl.pallas_call(
+        project_kernel,
+        out_shape=jax.ShapeDtypeStruct((listed, HP, NRAD), jnp.bfloat16),
+        in_specs=[smem, smem, smem, vmem, vmem, vmem, vmem],
+        out_specs=vmem,
+        scratch_shapes=[
+            pltpu.VMEM((FLUSH * 4, pts), jnp.float32),
+            pltpu.SMEM((FLUSH,), jnp.int32),
+            pltpu.SMEM((1,), jnp.int32),
+            pltpu.VMEM((FLUSH * HP, pts), jnp.float32),
+            pltpu.VMEM((FLUSH, pts), jnp.float32),
+            pltpu.VMEM((YR * listed, NRAD), jnp.float32),
+        ],
+        compiler_params=pltpu.CompilerParams(vmem_limit_bytes=40 << 20),
+        name="project",
+    )(counts, codes, runs, blocks, *tables, green)
+
+
+def scatter_kernel(blocks_ref, lists_ref, rows_at, out_ref, acc_ref):
+    devices, _, _, listed = blocks_ref.shape
+    wide = 256
+    acc_ref[...] = jnp.zeros_like(acc_ref)
+    column = lax.broadcasted_iota(jnp.int32, (wide, listed), 0)
+    groups = acc_ref.shape[0] // 16
+
+    @pl.loop(0, devices // 4)
+    def _(g):
+        total = acc_ref[...]
+        for v in range(4):
+            q = g * 4 + v
+            ids = lists_ref[pl.ds(q, 1), :]
+            target = (column == lax.bitwise_and(ids, wide - 1)).astype(jnp.bfloat16)
+            group = lax.shift_right_logical(ids, 8)
+            tiles = [blocks_ref[q, rows_at + m] for m in range(3)]
+            mom = jnp.concatenate(tiles + [jnp.zeros((4, listed), jnp.float32)], axis=0)
+            masked = jnp.concatenate(
+                [jnp.where(group == h, mom, 0.0) for h in range(groups)], axis=0
+            )
+            high = masked.astype(jnp.bfloat16)
+            low = (masked - high.astype(jnp.float32)).astype(jnp.bfloat16)
+            for part in (high, low):
+                total = total + lax.dot_general(
+                    part, target, (((1,), (1,)), ((), ())), preferred_element_type=jnp.float32
+                )
+        acc_ref[...] = total
+
+    for h in range(groups):
+        out_ref[:, h * wide : (h + 1) * wide] = acc_ref[h * 16 + 1 : h * 16 + 10, :]
+
+
+def scatter_moments(blocks, lists, atoms):
+    return pl.pallas_call(
+        lambda b, l, o, a: scatter_kernel(b, l, blocks.shape[1] - 3, o, a),
+        out_shape=jax.ShapeDtypeStruct((9, atoms), jnp.float32),
+        scratch_shapes=[pltpu.VMEM((atoms // 256 * 16, 256), jnp.float32)],
+        compiler_params=pltpu.CompilerParams(vmem_limit_bytes=40 << 20),
+        name="scatter_moments",
+    )(blocks, lists)
+
+
+def entry_tables(lists, my_list):
+    devices, listed = lists.shape
+    same = lists[:, :, None] == my_list[None, None, :]
+    slot = jnp.arange(1, listed + 1, dtype=jnp.int32)[None, :, None]
+    held = jnp.sum(jnp.where(same, slot, 0), axis=1)
+    present = held > 0
+    order = jnp.arange(devices)
+    rank = jnp.dot(
+        (order[None, :] < order[:, None]).astype(jnp.bfloat16),
+        present.astype(jnp.bfloat16),
+        preferred_element_type=jnp.float32,
+    ).astype(jnp.int32)
+    rank = jnp.where(present, rank, devices)
+    code = order[:, None].astype(jnp.int32) * listed + held - 1
+    picked = rank[None, :, :] == order[:, None, None]
+    codes = jnp.sum(jnp.where(picked, code[None], 0), axis=1)
+    return jnp.sum(present.astype(jnp.int32), axis=0), codes
+
+
 def per_device(
     grid_points,
     weighted_density,
@@ -379,88 +754,26 @@
     green,
     moment_table,
 ):
-    count_x = lax.axis_size("sx")
     count_y = lax.axis_size("sy")
-    devices = count_x * count_y
+    devices = lax.axis_size("sx") * count_y
     myself = lax.axis_index("sx") * count_y + lax.axis_index("sy")
-    all_lists = slot_atom.reshape(devices, -1)
-    listed = all_lists.shape[1]
-    capacity = 2 * listed // devices
-    total_atoms = atom_pos.shape[1]
-    my_list = all_lists[myself]
-    batches = near_slot.shape[0]
-    near_count = near_slot.shape[1]
-    batch_pts = grid_points.shape[1] // batches
-    block = math.gcd(batches, 4)
-    groups = batches // block
-    group_points = jnp.moveaxis(grid_points.reshape(3, groups, block * batch_pts), 1, 0)
-    group_density = weighted_density.reshape(groups, block * batch_pts)
-    group_slots = point_slot.reshape(groups, block * batch_pts)
-    group_near = near_slot.reshape(groups, block, near_count)
-    width = HARM * NRAD
-
-    def project_step(total, inputs):
-        points, density, slot_of_point = inputs
-        return (
-            total + project_points(points, density, slot_of_point, my_list, atom_pos, decay_rates),
-            None,
-        )
-
-    summed, unused = lax.scan(
-        project_step,
-        jnp.zeros((listed, width), jnp.float32),
-        (group_points, group_density, group_slots),
-    )
-    partial_value = summed.astype(jnp.bfloat16)
-    owner_ids = jnp.arange(devices)
-    counts = jnp.where(
-        owner_ids < devices // 4,
-        2 * OWN_AVG,
-        jnp.where(owner_ids < devices // 2, OWN_AVG, OWN_AVG // 2),
-    ).astype(jnp.int32)
-    range_ends = jnp.cumsum(counts)
-    starts = range_ends - counts
-    atom_index = jnp.arange(total_atoms)
-    owner = jnp.sum((range_ends[None, :] <= atom_index[:, None]).astype(jnp.int32), axis=1)
-    owners_all = owner[all_lists]
-    my_dest = owners_all[myself]
-    slot_index = jnp.arange(listed)
-    same_owner = (my_dest[:, None] == my_dest[None, :]) & (
-        slot_index[None, :] < slot_index[:, None]
-    )
-    earlier = jnp.sum(same_owner.astype(jnp.int32), axis=1)
-    send_row = my_dest * capacity + earlier
-    packing = (jnp.arange(devices * capacity)[:, None] == send_row[None, :]).astype(jnp.bfloat16)
-    outgoing = jnp.dot(packing, partial_value, preferred_element_type=jnp.float32).astype(
-        jnp.bfloat16
-    )
-    mine = owners_all == myself
-    recv_rank = jnp.cumsum(mine.astype(jnp.int32), axis=1) - 1
-    target = jnp.where(mine, owner_ids[:, None] * capacity + recv_rank, devices * capacity)
-    local_ids = jnp.where(mine, all_lists - starts[myself], OWN)
-    row_owned = (
-        jnp.full((devices * capacity + 1,), OWN, jnp.int32)
-        .at[target.reshape(-1)]
-        .set(local_ids.reshape(-1))[: devices * capacity]
-    )
-    incoming = lax.all_to_all(outgoing, ("sx", "sy"), split_axis=0, concat_axis=0, tiled=True)
-    selector = (row_owned[None, :] == jnp.arange(OWN)[:, None]).astype(jnp.bfloat16)
-    coeff_own = jnp.dot(selector, incoming, preferred_element_type=jnp.float32).reshape(
-        OWN, HARM, NRAD
-    )
-    pot_own = apply_green(coeff_own, green).astype(jnp.bfloat16).reshape(OWN, width)
-    moments_own = low_moments(coeff_own, moment_table)
-    reply = jnp.dot(selector.T, pot_own, preferred_element_type=jnp.float32).astype(jnp.bfloat16)
-    returned = lax.all_to_all(reply, ("sx", "sy"), split_axis=0, concat_axis=0, tiled=True)
-    gathered = lax.all_gather(moments_own, ("sx", "sy"), axis=1, tiled=True)
-    column = owner * OWN + atom_index - starts[owner]
-    moments_all = gathered[:, column]
-    slot_pot = jnp.dot(packing.T, returned, preferred_element_type=jnp.float32).astype(jnp.bfloat16)
-    padded = jnp.pad(slot_pot.reshape(listed, HARM, NRAD), ((0, 0), (0, HP - HARM), (0, 0)))
-    slot_table = jnp.concatenate([atom_pos[:, my_list], moments_all[:, my_list]], axis=0).T
+    lists = slot_atom.reshape(devices, -1)
+    my_list = lists[myself]
+    atoms = atom_pos.shape[1]
+    pts = grid_points.shape[1] // near_slot.shape[0]
+    tables = radial_tables(decay_rates, pts)
+    places = atom_pos[:, my_list]
+    mine = point_blocks(grid_points, weighted_density, point_slot, places, tables, moment_table)
+    gathered = gather_blocks(mine)
+    blocks = gathered.reshape((devices,) + mine.shape)
+    counts, codes = entry_tables(lists, my_list)
+    runs = blocks[:, mine.shape[0] - 3, 0, :].astype(jnp.int32)
+    slot_pot = project(counts, codes, runs, blocks, tables, green)
+    moments = scatter_moments(blocks, lists, atoms)
+    slot_table = jnp.concatenate([places, moments[:, my_list]], axis=0).T
     slot_table = jnp.pad(slot_table, ((0, 0), (0, 128 - slot_table.shape[1])))
     return evaluate(
-        grid_points, near_slot, slot_table, padded, atom_pos, moments_all, decay_rates
+        grid_points, near_slot, slot_table, slot_pot, atom_pos, moments, decay_rates
     )
 
 

time: 498 us -> 240 us (0.48)
  local copies, waits for them, and re-layouts: 249 us -> 10.3 us
  Pallas kernels: 87.7 us -> 218 us
  blocking collectives: 78.4 us -> 0 us
  matrix products: 29.2 us -> 0.14 us
  starting transfers between devices: 21.2 us -> 0 us
  other arithmetic: 28.6 us -> 8.69 us
    gather x20 -> x2, local copies, waits for them, and re-layouts: 141 us -> 1.88 us  [the longest x1 1.23 us: per_device(): slot_table = jnp.concatenate([places, moments[:, my_list]], axis=0).T]
    pallas_call x0 -> x4, Pallas kernels: none -> 130 us  [the longest x1 82 us: project(): pl.pallas_call(project_kernel, out_shape=jax.ShapeDtypeStruct((listed, HP...]
    all_gather x1 -> x0, blocking collectives: 78.4 us -> none  [per_device(): gathered = lax.all_gather(moments_own, ('sx', 'sy'), axis=1, tiled=True)]
    scatter x1 -> x0, local copies, waits for them, and re-layouts: 60.5 us -> none  [per_device(): row_owned = jnp.full((devices * capacity + 1,), OWN, jnp.int32).at[target...]
    dot_general x16 -> x1, matrix products: 29.2 us -> 0.14 us  [entry_tables(): jnp.dot((order[None, :] < order[:, None]).astype(jnp.bfloat16), present.a...]
    all_to_all x2 -> x0, starting transfers between devices: 21.2 us -> none  [the longest x1 11.5 us: per_device(): lax.all_to_all(outgoing, ('sx', 'sy'), split_axis=0, concat_axis=0, tiled...]
    all_to_all x5 -> x0, local copies, waits for them, and re-layouts: 19.9 us -> none  [the longest x3 14.4 us: per_device(): lax.all_to_all(outgoing, ('sx', 'sy'), split_axis=0, concat_axis=0, tiled...]
    another operation x8 -> x0, local copies, waits for them, and re-layouts: 11.8 us -> none  [harmonic_table(): return jnp.stack(stacked)]
  transfers between devices with their start and end apart: 2 -> 0, of which waited for: 0 -> 0; matrix products, arithmetic and copies ran while one was open for 19% -> 0% of each run, Pallas kernels for 0% -> 0%
where the time goes in v2:
time: 240 us; the launch traced here: 237 us
  Pallas kernels  218 us (91%)
  local copies, waits for them, and re-layouts  10.3 us (4%)
  other arithmetic  8.69 us (4%)
    pallas_call x1, Pallas kernels, evaluate(): pl.pallas_call(evaluate_kernel, out_shape=jax.ShapeDtypeStruct((batches,...  87.6 us
    pallas_call x1, Pallas kernels, project(): pl.pallas_call(project_kernel, out_shape=jax.ShapeDtypeStruct((listed, HP...  82 us
    pallas_call x1, Pallas kernels, gather_blocks(): pl.pallas_call(functools.partial(gather_kernel, cuts), out_shape=jax.Shap...  30.5 us
    pallas_call x1, Pallas kernels, scatter_moments(): pl.pallas_call(lambda b, l, o, a: scatter_kernel(b, l, blocks.shape[1] -...  11.1 us
    pallas_call x1, Pallas kernels, point_blocks(): pl.pallas_call(point_blocks_kernel, out_shape=jax.ShapeDtypeStruct((rows,...  6.68 us
    unnamed x20, local copies, waits for them, and re-layouts  5.76 us

profile of v2, /device:TPU:1, one launch (start us, length us, event | category | flops | bytes accessed | tf_op | source)
XLA Modules:
  0.0 237.2 jit_solution(4921342321409006733)
XLA Ops:
  0.0 0.0 copy-start.1
  0.0 0.7 fusion.2
  0.8 4.0 %select_reduce_fusion.1 = s32[128,128]{1,0:T(8,128)S(1)} fusion(s32[128]{0:T(128)S(1)} %iota_add_fusion, s32[128]{0:T(128)S(1)} %fusion.2, s32[128,128]{1,0:T(8,128)} %bitcast.22), kind=kLoop, calls=%fused_computation.4 | loop fusion | flops 6275072 | bytes 132096 | tf_op jit(solution)/shard_map/reduce_sum | solution.py:731
  4.8 0.1 convert_reduce_fusion
  4.9 0.1 fusion
  5.0 1.2 select_reduce_fusion.codes_ref
  6.3 0.7 fusion.1
  7.0 1.1 copy.18
  8.1 0.6 gather_fusion
  8.7 0.1 copy.21
  8.8 0.1 broadcast_in_dim.34.centre_ref
  8.9 0.7 sqrt_multiply_fusion
  9.6 0.1 broadcast_in_dim.35.rate_ref
  9.7 0.7 pad.12.table_ref
  10.4 0.0 copy-start.3
  10.4 0.8 copy-done.3
  11.1 0.0 copy-start.7
  11.1 0.7 copy-done.7
  11.8 0.0 copy-start.8
  11.8 0.7 copy-done.8
  12.5 6.7 %point_blocks.1 = f32[76,128]{1,0:T(8,128)S(1)} custom-call(f32[3,2048]{1,0:T(4,128)S(1)} %copy-done.3, f32[1,2048]{1,0:T(1,128)S(1)} %bitcast.27, s32[1,2048]{1,0:T(1,128)S(1)} %bitcast.28, f32[8,128]{1,0:T(8,128)S(1)} %pad.11.clone.places_ref, f32[128,128]{1,0:T(8,128)S(1)} %broadcast_in_dim.34.centre_ref, f32[128,128]{1,0:T(8,128)S(1)} %broadcast_in_dim.35.rate_ref, ...), custom_call_target="tpu_custom_call" | custom-call | tf_op jit(solution)/shard_map/point_blocks/pallas_call | solution.py:393
  19.2 0.7 reshape.89.mine_ref
  19.9 30.5 %gather_blocks.1 = f32[4,2,4,4,19,4,128]{6,5,4,3,2,1,0:T(4,128)} custom-call(f32[19,4,128]{2,1,0:T(4,128)} %reshape.89.mine_ref), custom_call_target="tpu_custom_call" | custom-call | tf_op jit(solution)/shard_map/gather_blocks/pallas_call | solution.py:499
  50.3 0.0 copy-start.2
  50.3 1.0 slice_convert_fusion
  51.4 0.0 copy-done.1
  51.4 0.0 copy-start
  51.4 2.4 %copy-done = f32[4,2,4,4,19,4,128]{6,5,4,3,2,1,0:T(4,128)S(1)} copy-done((f32[4,2,4,4,19,4,128]{6,5,4,3,2,1,0:T(4,128)S(1)}, f32[4,2,4,4,19,4,128]{6,5,4,3,2,1,0:T(4,128)}, u32[]{:S(2)}) %copy-start) | copy-done | bytes 4980760
  53.8 82.0 %project.1.slot_pot_ref = bf16[128,64,128]{2,1,0:T(8,128)(2,1)S(1)} custom-call(s32[128]{0:T(128)S(1)} %get-tuple-element.5.counts_ref, s32[128,128]{1,0:T(8,128)S(1)} %select_reduce_fusion.codes_ref, s32[128,128]{1,0:T(8,128)S(1)} %bitcast.25, f32[128,19,4,128]{3,2,1,0:T(4,128)S(1)} %bitcast.19, f32[128,128]{1,0:T(8,128)S(1)} %broadcast_in_dim.34.centre_ref, ...), custom_call_target="tpu_custom_call" | custom-call | tf_op jit(solution)/shard_map/project/pallas_call | solution.py:667
  135.9 0.0 copy-done.2
  135.9 0.0 copy-start.4
  135.9 0.0 copy-start.5
  135.9 0.0 copy-start.6
  135.9 11.1 %scatter_moments.1.moments_ref = f32[9,2048]{1,0:T(8,128)S(1)} custom-call(f32[128,19,4,128]{3,2,1,0:T(4,128)S(1)} %bitcast.20, s32[128,128]{1,0:T(8,128)S(1)} %bitcast.24), custom_call_target="tpu_custom_call" | custom-call | tf_op jit(solution)/shard_map/scatter_moments/pallas_call | solution.py:718
  147.0 0.4 copy.20
  147.3 1.2 gather_fusion.1
  148.6 0.9 maximum_bitcast_fusion
  149.5 0.0 copy-done.4
  149.5 0.0 copy-done.5
  149.5 0.0 copy-done.6
  149.5 87.6 %evaluate.1 = f32[16,1,128]{2,1,0:T(1,128)} custom-call(s32[16,64]{1,0:T(8,128)S(1)} %copy-done.6, s32[16,1,64]{2,1,0:T(1,128)S(1)} %bitcast.26, f32[3,2048]{1,0:T(4,128)S(1)} %copy-done.4, f32[128,128]{1,0:T(8,128)S(1)} %pad.13.slot_table_ref, bf16[128,64,128]{2,1,0:T(8,128)(2,1)S(1)} %project.1.slot_pot_ref, f32[3,2048]{1,0:T(4,128)S(1)} %copy-done.5, ...), custom_call_target="tpu_custom_call" | custom-call | tf_op jit(solution)/shard_map/evaluate/pallas_call | solution.py:245
  (6 shorter events, 0.0 us)
Async XLA Ops:
  0.0 51.4 %copy-start.1 = (f32[7,128,128]{2,1,0:T(8,128)S(1)}, f32[7,128,128]{2,1,0:T(8,128)}, u32[]{:S(2)}) copy-start(f32[7,128,128]{2,1,0:T(8,128)} %green_ref.1) | copy-start | bytes 1376260
  10.4 0.8 copy-start.3
  11.1 0.7 copy-start.7
  11.8 0.7 copy-start.8
  50.3 85.5 %copy-start.2 = (s32[16384]{0:T(1024)S(1)}, s32[16384]{0:T(1024)}, u32[]{:S(2)}) copy-start(s32[16384]{0:T(1024)} %param.13) | copy-start | bytes 196612
  51.4 2.4 %copy-start = (f32[4,2,4,4,19,4,128]{6,5,4,3,2,1,0:T(4,128)S(1)}, f32[4,2,4,4,19,4,128]{6,5,4,3,2,1,0:T(4,128)}, u32[]{:S(2)}) copy-start(f32[4,2,4,4,19,4,128]{6,5,4,3,2,1,0:T(4,128)} %gather_blocks.1) | copy-start | bytes 14942212
  135.9 13.6 %copy-start.4 = (f32[3,2048]{1,0:T(4,128)S(1)}, f32[3,2048]{1,0:T(4,128)}, u32[]{:S(2)}) copy-start(f32[3,2048]{1,0:T(4,128)} %points_ref.3) | copy-start | bytes 73732
  135.9 13.6 %copy-start.5 = (f32[3,2048]{1,0:T(4,128)S(1)}, f32[3,2048]{1,0:T(4,128)}, u32[]{:S(2)}) copy-start(f32[3,2048]{1,0:T(4,128)} %atoms_ref.1) | copy-start | bytes 73732
  135.9 13.6 %copy-start.6 = (s32[16,64]{1,0:T(8,128)S(1)}, s32[16,64]{1,0:T(8,128)}, u32[]{:S(2)}) copy-start(s32[16,64]{1,0:T(8,128)} %near_smem.1) | copy-start | bytes 12292

commit v3 on v2

--- a/solution.py
+++ b/solution.py
@@ -65,6 +65,31 @@
     return high, middle, rest - middle
 
 
+SPACING = 27.0 / (NRAD - 1)
+SHELL_ROWS = 16
+
+
+def radial_values(rho, first_ref, rate_ref, dtype=jnp.bfloat16):
+    rows, pts = first_ref.shape[0], rho.shape[1]
+    base = jnp.broadcast_to(rho, (rows, pts)) - first_ref[...]
+    pieces = []
+    for k in range(0, NRAD, rows):
+        e = base - (SPACING * k)
+        power = (e * e) * rate_ref[k : k + rows, :]
+        pieces.append(jnp.exp2(power.astype(dtype)))
+    return jnp.concatenate(pieces, axis=0)
+
+
+def radial_tables(decay_rates, width):
+    centres, spacing = shell_layout(decay_rates)
+    factor = decay_rates * (-math.log2(math.e) / spacing**2)
+    return (
+        jnp.broadcast_to(centres[:SHELL_ROWS, None], (SHELL_ROWS, width)),
+        jnp.broadcast_to(factor[:, None], (decay_rates.shape[0], width)),
+    )
+
+
+FARC = 8
 FEATURES = 9
 FEATURE_ROWS = 6 * FEATURES + 3
 FAR_ROWS = 64
@@ -130,7 +155,7 @@
     slot_pot_ref,
     atoms_ref,
     moments_ref,
-    centre_ref,
+    first_ref,
     rate_ref,
     out_ref,
     far_rows,
@@ -157,12 +182,11 @@
     far_acc[...] = jnp.zeros_like(far_acc)
     chunk = 256
 
-    @pl.loop(0, atoms // chunk)
-    def _(c):
-        base = pl.multiple_of(c * chunk, chunk)
+    for c in range(FARC):
+        base = c * chunk
 
         def table(q):
-            return far_table[:, pl.ds(pl.multiple_of(q * atoms + base, chunk), chunk)]
+            return far_table[:, q * atoms + base : q * atoms + base + chunk]
 
         square = jnp.dot(features, table(0), preferred_element_type=jnp.float32)
         linear = jnp.dot(features, table(1), preferred_element_type=jnp.float32)
@@ -209,15 +233,13 @@
         corr = corr + inv * (term[0] + inv * (degree1 + inv * degree2))
     corr_ref[...] = corr
 
-    centre, rate = centre_ref[...], rate_ref[...]
-    unroll = 4
+    unroll = 32
 
     def pairs(g, total):
         for v in range(unroll):
             j = g * unroll + v
             coefs = slot_pot_ref[near_smem[b, j]]
-            t = (rho_rows[pl.ds(j, 1), :] - centre) * rate
-            radial = jnp.exp2(-(t * t)).astype(jnp.bfloat16)
+            radial = radial_values(rho_rows[pl.ds(j, 1), :], first_ref, rate_ref)
             values = jnp.dot(coefs, radial, preferred_element_type=jnp.float32)
             rows = y_rows[pl.ds(pl.multiple_of(j * YR, YR), YR), :]
             total = total + values[0:YR] * rows
@@ -234,10 +256,7 @@
     batches, near_count = near_slot.shape
     pts = points.shape[1] // batches
     atoms = atom_pos.shape[1]
-    centres, spacing = shell_layout(decay_rates)
-    rate = jnp.sqrt(decay_rates * math.log2(math.e)) / spacing
-    centre_full = jnp.broadcast_to(centres[:, None], (NRAD, pts))
-    rate_full = jnp.broadcast_to(rate[:, None], (NRAD, pts))
+    first, factor = radial_tables(decay_rates, pts)
 
     def whole(shape):
         return pl.BlockSpec(shape, lambda b, near: (0,) * len(shape))
@@ -255,8 +274,8 @@
                 whole(slot_pot.shape),
                 whole(atom_pos.shape),
                 whole(moments.shape),
-                whole((NRAD, pts)),
-                whole((NRAD, pts)),
+                whole(first.shape),
+                whole(factor.shape),
             ],
             out_specs=pl.BlockSpec((1, 1, pts), lambda b, near: (b, 0, 0)),
             scratch_shapes=[
@@ -281,8 +300,8 @@
         slot_pot,
         atom_pos,
         moments,
-        centre_full,
-        rate_full,
+        first,
+        factor,
     )
     return out.reshape(-1)
 
@@ -292,7 +311,7 @@
     density_ref,
     slots_ref,
     places_ref,
-    centre_ref,
+    first_ref,
     rate_ref,
     table_ref,
     out_ref,
@@ -300,7 +319,7 @@
     q_rows,
 ):
     listed = places_ref.shape[1]
-    pts = centre_ref.shape[1]
+    pts = first_ref.shape[1]
     blocks = points_ref.shape[1] // pts
     slot_rows = lax.broadcasted_iota(jnp.int32, (listed, pts), 0)
     lane = lax.broadcasted_iota(jnp.int32, (listed, pts), 1)
@@ -355,8 +374,7 @@
         square = dx * dx + dy * dy + dz * dz + 1.0
         inv = lax.rsqrt(square)
         rho = square * inv
-        t = (rho - centre_ref[...]) * rate_ref[...]
-        radial = jnp.exp2(-(t * t))
+        radial = radial_values(rho, first_ref, rate_ref, jnp.float32)
         levels = jnp.dot(
             table_ref[...], radial, precision=lax.Precision.HIGHEST, preferred_element_type=jnp.float32
         )
@@ -377,13 +395,6 @@
     out_ref[4 * blocks : 4 * blocks + 1, :] = packed.T[0:1, :]
     out_ref[4 * blocks + 1 : 4 * blocks + 10, :] = moments[0:9]
     out_ref[4 * blocks + 10 : 4 * blocks + 12, :] = jnp.zeros((2, listed), jnp.float32)
-
-
-def radial_tables(decay_rates, width):
-    centres, spacing = shell_layout(decay_rates)
-    rate = jnp.sqrt(decay_rates * math.log2(math.e)) / spacing
-    shape = (decay_rates.shape[0], width)
-    return jnp.broadcast_to(centres[:, None], shape), jnp.broadcast_to(rate[:, None], shape)
 
 
 def point_blocks(points, density, slots, places, tables, moment_table):
@@ -515,37 +526,90 @@
 
 CHUNK = 32
 PER = 4
-FLUSH = 8
+GROUP = 8
 
 
 def project_kernel(
+    total_ref,
+    plan_ref,
     counts_ref,
     codes_ref,
     runs_ref,
     blocks_ref,
-    centre_ref,
+    first_ref,
     rate_ref,
     green_ref,
     pot_ref,
     buffer,
     owner_ref,
-    used_ref,
+    extra_ref,
+    extra_run,
+    extra_from,
     y_rows,
     rho_rows,
     coefs_ref,
 ):
     listed = counts_ref.shape[0]
-    pts = centre_ref.shape[1]
+    pts = first_ref.shape[1]
     coefs_ref[...] = jnp.zeros_like(coefs_ref)
     y_rows[...] = jnp.zeros_like(y_rows)
+    buffer[...] = jnp.zeros_like(buffer)
+    for f in range(2 * GROUP):
+        owner_ref[f] = 0
+    extra_ref[0] = 0
     lane = lax.broadcasted_iota(jnp.int32, (4, pts), 1)
-    used_ref[0] = 0
-    for f in range(FLUSH):
-        owner_ref[f] = 0
-
-    def flush():
+
+    def piece(device, start, length, position):
+        at = lax.shift_right_logical(start, 7)
+        off = lax.bitwise_and(start, 127)
+        value = jnp.where(lane >= off, blocks_ref[device, at], blocks_ref[device, at + 1])
+        left = position * CHUNK
+        moved = pltpu.roll(value, lax.bitwise_and(left - off + 128, 127), 1)
+        keep = (lane >= left) & (lane < left + length)
+        return jnp.where(keep, moved, 0.0)
+
+    def collect(g, half):
+        owners, values, runs = [], [], []
+        longest = jnp.int32(0)
+        for f in range(GROUP):
+            plan = plan_ref[g * GROUP + f]
+            j = lax.shift_right_logical(plan, 12)
+            r = lax.bitwise_and(plan, 4095)
+            count = jnp.where(g * GROUP + f < total_ref[0], counts_ref[j], 0)
+            owners.append(j)
+            value = None
+            for v in range(PER):
+                code = codes_ref[r + v, j]
+                device = lax.shift_right_logical(code, 7)
+                run = runs_ref[device, lax.bitwise_and(code, 127)]
+                length = jnp.where(r + v < count, lax.bitwise_and(run, 4095), 0)
+                start = lax.shift_right_logical(run, 12)
+                longest = jnp.maximum(longest, length)
+                part = piece(device, start, jnp.minimum(length, CHUNK), v)
+                value = part if value is None else value + part
+                runs.append((device, start, length, j))
+            values.append(value)
+        for f in range(GROUP):
+            row = half * GROUP + f
+            buffer[pl.ds(row * 4, 4), :] = values[f]
+            owner_ref[row] = owners[f]
+        return longest, runs
+
+    def note(longest, runs):
+        @pl.when(longest > CHUNK)
+        def _():
+            for device, start, length, j in runs:
+
+                @pl.when(length > CHUNK)
+                def _():
+                    at = extra_ref[0]
+                    extra_run[at] = start * 4096 + length
+                    extra_from[at] = device * 4096 + j
+                    extra_ref[0] = at + 1
+
+    def flush(half):
         def component(c):
-            return buffer[pl.ds(c, FLUSH, stride=4), :]
+            return buffer[pl.ds(half * (4 * GROUP) + c, GROUP, stride=4), :]
 
         dx, dy, dz, weight = (component(c) for c in range(4))
         square = dx * dx + dy * dy + dz * dz + 1.0
@@ -553,89 +617,61 @@
         rho_rows[...] = square * inv
 
         def emit(i, value):
-            y_rows[pl.ds(i, FLUSH, stride=HP), :] = value * weight
+            y_rows[pl.ds(i, GROUP, stride=HP), :] = value * weight
 
         harmonic_rows(dx * inv, dy * inv, dz * inv, 6, emit)
         sums = []
-        for f in range(FLUSH):
-            t = (rho_rows[f : f + 1, :] - centre_ref[...]) * rate_ref[...]
-            radial = jnp.exp2(-(t * t)).astype(jnp.bfloat16)
+        for f in range(GROUP):
+            radial = radial_values(rho_rows[f : f + 1, :], first_ref, rate_ref)
             rows = y_rows[f * HP : (f + 1) * HP, :].astype(jnp.bfloat16)
             sums.append(
                 lax.dot_general(
                     rows, radial, (((1,), (1,)), ((), ())), preferred_element_type=jnp.float32
                 )
             )
-        for f in range(FLUSH):
-            at = pl.ds(owner_ref[f], YR, stride=listed)
+        for f in range(GROUP):
+            at = pl.ds(pl.multiple_of(owner_ref[half * GROUP + f] * YR, 8), YR)
             coefs_ref[at, :] = coefs_ref[at, :] + sums[f][0:YR]
+
+    groups = (total_ref[0] + (GROUP - 1)) // GROUP
+    note(*collect(0, 0))
+
+    @pl.loop(0, groups)
+    def _(g):
+        half = lax.bitwise_and(g, 1)
+        later = jnp.minimum(g + 1, groups - 1)
+        longest, runs = collect(later, 1 - half)
+        flush(half)
+        note(jnp.where(later > g, longest, 0), runs)
+
+    @pl.when(extra_ref[0] > 0)
+    def _():
         buffer[...] = jnp.zeros_like(buffer)
-        used_ref[0] = 0
-
-    buffer[...] = jnp.zeros_like(buffer)
-
-    def window(device, start):
-        at = lax.shift_right_logical(start, 7)
-        off = lax.bitwise_and(start, 127)
-        first = blocks_ref[device, at]
-        second = blocks_ref[device, at + 1]
-        return jnp.where(lane >= off, first, second), off
-
-    def piece(device, start, length, position):
-        value, off = window(device, start)
-        left = position * CHUNK
-        moved = pltpu.roll(value, lax.bitwise_and(left - off + 128, 127), 1)
-        keep = (lane >= left) & (lane < left + length)
-        return jnp.where(keep, moved, 0.0)
-
-    def put(j, value):
-        row = used_ref[0]
-        buffer[pl.ds(row * 4, 4), :] = value
-        owner_ref[row] = j
-        used_ref[0] = row + 1
-
-        @pl.when(row + 1 == FLUSH)
-        def _():
-            flush()
-
-    @pl.loop(0, listed)
-    def _(j):
-        count = counts_ref[j]
-
-        @pl.loop(0, lax.shift_right_logical(count + (PER - 1), 2))
-        def _(g):
-            total = jnp.zeros((4, pts), jnp.float32)
-            longest = jnp.int32(0)
-            entries = []
-            for v in range(PER):
-                r = g * PER + v
-                code = codes_ref[r, j]
-                device = lax.shift_right_logical(code, 7)
-                run = runs_ref[device, lax.bitwise_and(code, 127)]
-                length = jnp.where(r < count, lax.bitwise_and(run, 4095), 0)
-                start = lax.shift_right_logical(run, 12)
-                entries.append((device, start, length))
-                longest = jnp.maximum(longest, length)
-                total = total + piece(device, start, jnp.minimum(length, CHUNK), v)
-            put(j, total)
-
-            @pl.when(longest > CHUNK)
-            def _():
-                for device, start, length in entries:
-
-                    @pl.loop(1, (length + (CHUNK - 1)) // CHUNK)
-                    def _(c):
-                        put(
-                            j,
-                            piece(
-                                device,
-                                start + c * CHUNK,
-                                jnp.minimum(length - c * CHUNK, CHUNK),
-                                0,
-                            ),
-                        )
-
-    flush()
+        extra_ref[1] = 0
+
+        @pl.loop(0, extra_ref[0])
+        def _(n):
+            run, source = extra_run[n], extra_from[n]
+            device, j = lax.shift_right_logical(source, 12), lax.bitwise_and(source, 4095)
+            start = lax.shift_right_logical(run, 12) + CHUNK
+            length = lax.bitwise_and(run, 4095) - CHUNK
+
+            @pl.loop(0, lax.shift_right_logical(length + (pts - 1), 7))
+            def _(c):
+                row = extra_ref[1]
+                part = piece(device, start + c * pts, jnp.minimum(length - c * pts, pts), 0)
+                buffer[pl.ds(row * 4, 4), :] = part
+                owner_ref[row] = j
+                extra_ref[1] = row + 1
+
+                @pl.when(row + 1 == GROUP)
+                def _():
+                    flush(0)
+                    buffer[...] = jnp.zeros_like(buffer)
+                    extra_ref[1] = 0
+
+        flush(0)
+
     for l in range(7):
         top = green_ref[l]
         high = top.astype(jnp.bfloat16)
@@ -643,20 +679,38 @@
         half = jnp.concatenate([high, low], axis=1)
         table = jnp.concatenate([half, half], axis=0)
         for i in range(l * l, (l + 1) * (l + 1)):
-            rows = coefs_ref[i * listed : (i + 1) * listed, :]
+            at = pl.ds(i, listed, stride=YR)
+            rows = coefs_ref[at, :]
             big = rows.astype(jnp.bfloat16)
             small = (rows - big.astype(jnp.float32)).astype(jnp.bfloat16)
             both = jnp.dot(
                 jnp.concatenate([big, small], axis=1), table, preferred_element_type=jnp.float32
             )
-            coefs_ref[i * listed : (i + 1) * listed, :] = both[:, 0:128] + both[:, 128:256]
-
-    @pl.loop(0, listed)
-    def _(j):
-        rows = coefs_ref[pl.ds(j, YR, stride=listed), :]
-        pot_ref[j] = jnp.concatenate(
-            [rows, jnp.zeros((HP - YR, rows.shape[1]), jnp.float32)], axis=0
-        ).astype(jnp.bfloat16)
+            coefs_ref[at, :] = both[:, 0:128] + both[:, 128:256]
+
+    @pl.loop(0, listed // 8)
+    def _(g):
+        for v in range(8):
+            j = g * 8 + v
+            rows = coefs_ref[pl.ds(pl.multiple_of(j * YR, 8), YR), :]
+            pot_ref[j] = jnp.concatenate(
+                [rows, jnp.zeros((HP - YR, rows.shape[1]), jnp.float32)], axis=0
+            ).astype(jnp.bfloat16)
+
+
+def block_plan(counts, devices):
+    listed = counts.shape[0]
+    index = jnp.arange(listed)
+    needed = (counts + (PER - 1)) // PER
+    ends = jnp.sum(jnp.where(index[None, :] <= index[:, None], needed[None, :], 0), axis=1)
+    starts = ends - needed
+    most = listed * (devices // PER) + GROUP
+    block = jnp.arange(most)[:, None]
+    inside = (block >= starts[None, :]) & (block < ends[None, :])
+    value = index[None, :] * 4096 + (block - starts[None, :]) * PER
+    plan = jnp.sum(jnp.where(inside, value, 0), axis=1)
+    total = ends[listed - 1]
+    return total.reshape(1).astype(jnp.int32), plan.astype(jnp.int32)
 
 
 def project(counts, codes, runs, blocks, tables, green):
@@ -664,22 +718,25 @@
     pts = tables[0].shape[1]
     smem = pl.BlockSpec(memory_space=pltpu.SMEM)
     vmem = pl.BlockSpec(memory_space=pltpu.VMEM)
+    total, plan = block_plan(counts, codes.shape[0])
     return pl.pallas_call(
         project_kernel,
         out_shape=jax.ShapeDtypeStruct((listed, HP, NRAD), jnp.bfloat16),
-        in_specs=[smem, smem, smem, vmem, vmem, vmem, vmem],
+        in_specs=[smem] * 5 + [vmem] * 4,
         out_specs=vmem,
         scratch_shapes=[
-            pltpu.VMEM((FLUSH * 4, pts), jnp.float32),
-            pltpu.SMEM((FLUSH,), jnp.int32),
-            pltpu.SMEM((1,), jnp.int32),
-            pltpu.VMEM((FLUSH * HP, pts), jnp.float32),
-            pltpu.VMEM((FLUSH, pts), jnp.float32),
+            pltpu.VMEM((2 * GROUP * 4, pts), jnp.float32),
+            pltpu.SMEM((2 * GROUP,), jnp.int32),
+            pltpu.SMEM((2,), jnp.int32),
+            pltpu.SMEM((codes.size,), jnp.int32),
+            pltpu.SMEM((codes.size,), jnp.int32),
+            pltpu.VMEM((GROUP * HP, pts), jnp.float32),
+            pltpu.VMEM((GROUP, pts), jnp.float32),
             pltpu.VMEM((YR * listed, NRAD), jnp.float32),
         ],
         compiler_params=pltpu.CompilerParams(vmem_limit_bytes=40 << 20),
         name="project",
-    )(counts, codes, runs, blocks, *tables, green)
+    )(total, plan, counts, codes, runs, blocks, *tables, green)
 
 
 def scatter_kernel(blocks_ref, lists_ref, rows_at, out_ref, acc_ref):
@@ -687,38 +744,49 @@
     wide = 256
     acc_ref[...] = jnp.zeros_like(acc_ref)
     column = lax.broadcasted_iota(jnp.int32, (wide, listed), 0)
-    groups = acc_ref.shape[0] // 16
-
-    @pl.loop(0, devices // 4)
+    groups = acc_ref.shape[0] // 32
+
+    steps = 8
+
+    @pl.loop(0, devices // steps)
     def _(g):
         total = acc_ref[...]
-        for v in range(4):
-            q = g * 4 + v
-            ids = lists_ref[pl.ds(q, 1), :]
-            target = (column == lax.bitwise_and(ids, wide - 1)).astype(jnp.bfloat16)
-            group = lax.shift_right_logical(ids, 8)
-            tiles = [blocks_ref[q, rows_at + m] for m in range(3)]
-            mom = jnp.concatenate(tiles + [jnp.zeros((4, listed), jnp.float32)], axis=0)
-            masked = jnp.concatenate(
-                [jnp.where(group == h, mom, 0.0) for h in range(groups)], axis=0
+        for v in range(0, steps, 2):
+            targets, parts = [], []
+            for q in (g * steps + v, g * steps + v + 1):
+                ids = lists_ref[pl.ds(q, 1), :]
+                targets.append(
+                    (column == lax.bitwise_and(ids, wide - 1)).astype(jnp.bfloat16)
+                )
+                group = lax.shift_right_logical(ids, 8)
+                tiles = [blocks_ref[q, rows_at + m] for m in range(3)]
+                mom = jnp.concatenate(tiles + [jnp.zeros((4, listed), jnp.float32)], axis=0)
+                top = mom.astype(jnp.bfloat16).astype(jnp.float32)
+                both = [
+                    jnp.where(group == h, half, 0.0)
+                    for h in range(groups)
+                    for half in (top, mom - top)
+                ]
+                parts.append(jnp.concatenate(both, axis=0).astype(jnp.bfloat16))
+            total = total + lax.dot_general(
+                jnp.concatenate(parts, axis=1),
+                jnp.concatenate(targets, axis=1),
+                (((1,), (1,)), ((), ())),
+                preferred_element_type=jnp.float32,
             )
-            high = masked.astype(jnp.bfloat16)
-            low = (masked - high.astype(jnp.float32)).astype(jnp.bfloat16)
-            for part in (high, low):
-                total = total + lax.dot_general(
-                    part, target, (((1,), (1,)), ((), ())), preferred_element_type=jnp.float32
-                )
         acc_ref[...] = total
 
     for h in range(groups):
-        out_ref[:, h * wide : (h + 1) * wide] = acc_ref[h * 16 + 1 : h * 16 + 10, :]
+        out_ref[:, h * wide : (h + 1) * wide] = (
+            acc_ref[h * 32 + 1 : h * 32 + 10, :] + acc_ref[h * 32 + 17 : h * 32 + 26, :]
+        )
 
 
 def scatter_moments(blocks, lists, atoms):
     return pl.pallas_call(
         lambda b, l, o, a: scatter_kernel(b, l, blocks.shape[1] - 3, o, a),
         out_shape=jax.ShapeDtypeStruct((9, atoms), jnp.float32),
-        scratch_shapes=[pltpu.VMEM((atoms // 256 * 16, 256), jnp.float32)],
+        scratch_shapes=[pltpu.VMEM((atoms // 256 * 32, 256), jnp.float32)],
         compiler_params=pltpu.CompilerParams(vmem_limit_bytes=40 << 20),
         name="scatter_moments",
     )(blocks, lists)

time: 240 us -> 149 us (0.62); the launches traced: 237 us -> 149 us
  Pallas kernels: 218 us -> 128 us
    pallas_call x1, Pallas kernels: 87.6 us -> 34.6 us  [evaluate(): pl.pallas_call(evaluate_kernel, out_shape=jax.ShapeDtypeStruct((batches,...]
    pallas_call x1, Pallas kernels: 82 us -> 50.6 us  [project(): pl.pallas_call(project_kernel, out_shape=jax.ShapeDtypeStruct((listed, HP...]
    pallas_call x1, Pallas kernels: 11.1 us -> 5.65 us  [scatter_moments(): pl.pallas_call(lambda b, l, o, a: scatter_kernel(b, l, blocks.shape[1] -...]
where the time goes in v3:
time: 149 us
  Pallas kernels  128 us (86%)
  local copies, waits for them, and re-layouts  10.8 us (7%)
  other arithmetic  9.54 us (6%)
    pallas_call x1, Pallas kernels, project(): pl.pallas_call(project_kernel, out_shape=jax.ShapeDtypeStruct((listed, HP...  50.6 us
    pallas_call x1, Pallas kernels, evaluate(): pl.pallas_call(evaluate_kernel, out_shape=jax.ShapeDtypeStruct((batches,...  34.6 us
    pallas_call x1, Pallas kernels, gather_blocks(): pl.pallas_call(functools.partial(gather_kernel, cuts), out_shape=jax.Shap...  30.5 us
    pallas_call x1, Pallas kernels, point_blocks(): pl.pallas_call(point_blocks_kernel, out_shape=jax.ShapeDtypeStruct((rows,...  6.68 us
    unnamed x20, local copies, waits for them, and re-layouts  5.76 us
    pallas_call x1, Pallas kernels, scatter_moments(): pl.pallas_call(lambda b, l, o, a: scatter_kernel(b, l, blocks.shape[1] -...  5.65 us
    reduce_sum x1, other arithmetic, entry_tables(): held = jnp.sum(jnp.where(same, slot, 0), axis=1)  4.09 us

profile of v3, /device:TPU:1, one launch (start us, length us, event | category | flops | bytes accessed | tf_op | source)
XLA Modules:
  0.0 148.7 jit_solution(1771267783417327786)
XLA Ops:
  0.0 0.7 fusion.3
  0.7 4.1 %select_reduce_fusion.1 = s32[128,128]{1,0:T(8,128)S(1)} fusion(s32[128]{0:T(128)S(1)} %iota_add_fusion, s32[128]{0:T(128)S(1)} %fusion.3, s32[128,128]{1,0:T(8,128)} %bitcast.23), kind=kLoop, calls=%fused_computation.4 | loop fusion | flops 6275072 | bytes 132096 | tf_op jit(solution)/shard_map/reduce_sum | solution.py:799
  4.8 0.1 convert_reduce_fusion
  4.9 0.1 select_reduce_fusion.3
  5.0 0.7 select_reduce_fusion.2.plan_ref
  5.8 0.1 fusion.1
  5.9 1.2 select_reduce_fusion.codes_ref
  7.1 0.6 slice.15.total_ref
  7.7 0.7 fusion.2
  8.4 1.1 copy.18
  9.5 0.6 gather_fusion
  10.2 0.1 copy.21
  10.3 0.7 broadcast_multiply_fusion
  10.9 0.1 broadcast_in_dim.48.rate_ref
  11.0 0.1 broadcast_in_dim.47.first_ref
  11.1 0.7 pad.12.table_ref
  11.8 0.0 copy-start.4
  11.8 0.8 copy-done.4
  12.5 0.0 copy-start.7
  12.5 0.7 copy-done.7
  13.2 0.0 copy-start.8
  13.2 0.7 copy-done.8
  13.9 6.7 %point_blocks.1 = f32[76,128]{1,0:T(8,128)S(1)} custom-call(f32[3,2048]{1,0:T(4,128)S(1)} %copy-done.4, f32[1,2048]{1,0:T(1,128)S(1)} %bitcast.28, s32[1,2048]{1,0:T(1,128)S(1)} %bitcast.29, f32[8,128]{1,0:T(8,128)S(1)} %pad.11.clone.places_ref, f32[16,128]{1,0:T(8,128)S(1)} %broadcast_in_dim.47.first_ref, f32[128,128]{1,0:T(8,128)S(1)} %broadcast_in_dim.48.rate_ref, ...), custom_call_target="tpu_custom_call" | custom-call | tf_op jit(solution)/shard_map/point_blocks/pallas_call | solution.py:404
  20.6 0.7 reshape.113.mine_ref
  21.3 0.0 copy-start.1
  21.3 30.5 %gather_blocks.1 = f32[4,2,4,4,19,4,128]{6,5,4,3,2,1,0:T(4,128)} custom-call(f32[19,4,128]{2,1,0:T(4,128)} %reshape.113.mine_ref), custom_call_target="tpu_custom_call" | custom-call | tf_op jit(solution)/shard_map/gather_blocks/pallas_call | solution.py:510
  51.8 1.0 slice_convert_fusion
  52.8 0.0 copy-done.1
  52.8 0.0 copy-start
  52.8 2.4 %copy-done = f32[4,2,4,4,19,4,128]{6,5,4,3,2,1,0:T(4,128)S(1)} copy-done((f32[4,2,4,4,19,4,128]{6,5,4,3,2,1,0:T(4,128)S(1)}, f32[4,2,4,4,19,4,128]{6,5,4,3,2,1,0:T(4,128)}, u32[]{:S(2)}) %copy-start) | copy-done | bytes 4980760
  55.2 0.0 copy-start.2
  55.2 50.6 %project.1.slot_pot_ref = bf16[128,64,128]{2,1,0:T(8,128)(2,1)S(1)} custom-call(s32[1]{0:T(128)} %slice.15.total_ref, s32[4104]{0:T(1024)S(1)} %select_reduce_fusion.2.plan_ref, s32[128]{0:T(128)S(1)} %get-tuple-element.5.counts_ref, s32[128,128]{1,0:T(8,128)S(1)} %select_reduce_fusion.codes_ref, s32[128,128]{1,0:T(8,128)S(1)} %bitcast.26, ...), custom_call_target="tpu_custom_call" | custom-call | tf_op jit(solution)/shard_map/project/pallas_call | solution.py:722
  105.8 0.0 copy-done.2
  105.8 0.0 copy-start.3
  105.8 0.0 copy-start.5
  105.9 0.0 copy-start.6
  105.9 5.6 %scatter_moments.1.moments_ref = f32[9,2048]{1,0:T(8,128)S(1)} custom-call(f32[128,19,4,128]{3,2,1,0:T(4,128)S(1)} %bitcast.21, s32[128,128]{1,0:T(8,128)S(1)} %bitcast.25), custom_call_target="tpu_custom_call" | custom-call | tf_op jit(solution)/shard_map/scatter_moments/pallas_call | solution.py:786
  111.5 0.4 copy.20
  111.9 1.2 gather_fusion.1
  113.1 0.9 maximum_bitcast_fusion
  114.1 0.0 copy-done.3
  114.1 0.0 copy-done.5
  114.1 0.0 copy-done.6
  114.1 34.6 %evaluate.1 = f32[16,1,128]{2,1,0:T(1,128)} custom-call(s32[16,64]{1,0:T(8,128)S(1)} %copy-done.6, s32[16,1,64]{2,1,0:T(1,128)S(1)} %bitcast.27, f32[3,2048]{1,0:T(4,128)S(1)} %copy-done.5, f32[128,128]{1,0:T(8,128)S(1)} %pad.13.slot_table_ref, bf16[128,64,128]{2,1,0:T(8,128)(2,1)S(1)} %project.1.slot_pot_ref, f32[3,2048]{1,0:T(4,128)S(1)} %copy-done.3, ...), custom_call_target="tpu_custom_call" | custom-call | tf_op jit(solution)/shard_map/evaluate/pallas_call | solution.py:264
  (9 shorter events, 0.1 us)
Async XLA Ops:
  11.8 0.8 copy-start.4
  12.5 0.7 copy-start.7
  13.2 0.7 copy-start.8
  21.3 31.5 %copy-start.1 = (f32[7,128,128]{2,1,0:T(8,128)S(1)}, f32[7,128,128]{2,1,0:T(8,128)}, u32[]{:S(2)}) copy-start(f32[7,128,128]{2,1,0:T(8,128)} %green_ref.1) | copy-start | bytes 1376260
  52.8 2.4 %copy-start = (f32[4,2,4,4,19,4,128]{6,5,4,3,2,1,0:T(4,128)S(1)}, f32[4,2,4,4,19,4,128]{6,5,4,3,2,1,0:T(4,128)}, u32[]{:S(2)}) copy-start(f32[4,2,4,4,19,4,128]{6,5,4,3,2,1,0:T(4,128)} %gather_blocks.1) | copy-start | bytes 14942212
  55.2 50.6 %copy-start.2 = (s32[16384]{0:T(1024)S(1)}, s32[16384]{0:T(1024)}, u32[]{:S(2)}) copy-start(s32[16384]{0:T(1024)} %param.13) | copy-start | bytes 196612
  105.8 8.2 %copy-start.3 = (f32[3,2048]{1,0:T(4,128)S(1)}, f32[3,2048]{1,0:T(4,128)}, u32[]{:S(2)}) copy-start(f32[3,2048]{1,0:T(4,128)} %atoms_ref.1) | copy-start | bytes 73732
  105.8 8.2 %copy-start.5 = (f32[3,2048]{1,0:T(4,128)S(1)}, f32[3,2048]{1,0:T(4,128)}, u32[]{:S(2)}) copy-start(f32[3,2048]{1,0:T(4,128)} %points_ref.3) | copy-start | bytes 73732
  105.9 8.2 %copy-start.6 = (s32[16,64]{1,0:T(8,128)S(1)}, s32[16,64]{1,0:T(8,128)}, u32[]{:S(2)}) copy-start(s32[16,64]{1,0:T(8,128)} %near_smem.1) | copy-start | bytes 12292

commit v4 on v3

--- a/solution.py
+++ b/solution.py
@@ -200,12 +200,12 @@
     far_row = jnp.sum(far_acc[...].T, axis=0, keepdims=True)
 
     hot = (
-        lax.broadcasted_iota(jnp.int32, (slot_table_ref.shape[0], near_count), 0) == near_ref[0]
+        lax.broadcasted_iota(jnp.int32, (slot_table_ref.shape[1], near_count), 0) == near_ref[0]
     ).astype(jnp.float32)
     info = lax.dot_general(
         hot,
         slot_table_ref[...],
-        (((0,), (0,)), ((), ())),
+        (((0,), (1,)), ((), ())),
         precision=lax.Precision.HIGHEST,
         preferred_element_type=jnp.float32,
     )
@@ -411,9 +411,9 @@
         points,
         density.reshape(1, count),
         slots.reshape(1, count),
-        jnp.pad(places, ((0, 5), (0, 0))),
+        places,
         *tables,
-        jnp.pad(moment_table, ((0, 5), (0, 0))),
+        moment_table,
     )
     return out.reshape(rows // 4, 4, pts)
 
@@ -526,14 +526,16 @@
 
 CHUNK = 32
 PER = 4
-GROUP = 8
+LONG = 64
+GROUP = 16
 
 
 def project_kernel(
+    lists,
     total_ref,
     plan_ref,
-    counts_ref,
     codes_ref,
+    words_ref,
     runs_ref,
     blocks_ref,
     first_ref,
@@ -543,13 +545,13 @@
     buffer,
     owner_ref,
     extra_ref,
-    extra_run,
-    extra_from,
+    extra_code,
+    extra_owner,
     y_rows,
     rho_rows,
     coefs_ref,
 ):
-    listed = counts_ref.shape[0]
+    listed = codes_ref.shape[1]
     pts = first_ref.shape[1]
     coefs_ref[...] = jnp.zeros_like(coefs_ref)
     y_rows[...] = jnp.zeros_like(y_rows)
@@ -558,53 +560,52 @@
         owner_ref[f] = 0
     extra_ref[0] = 0
     lane = lax.broadcasted_iota(jnp.int32, (4, pts), 1)
-
-    def piece(device, start, length, position):
-        at = lax.shift_right_logical(start, 7)
-        off = lax.bitwise_and(start, 127)
-        value = jnp.where(lane >= off, blocks_ref[device, at], blocks_ref[device, at + 1])
-        left = position * CHUNK
-        moved = pltpu.roll(value, lax.bitwise_and(left - off + 128, 127), 1)
-        keep = (lane >= left) & (lane < left + length)
-        return jnp.where(keep, moved, 0.0)
+    held = blocks_ref.shape[0] // lists
+
+    def window(tile, off, left):
+        value = jnp.where(lane >= off, blocks_ref[tile], blocks_ref[tile + 1])
+        return pltpu.roll(value, lax.bitwise_and(left + 128 - off, 127), 1)
 
     def collect(g, half):
-        owners, values, runs = [], [], []
-        longest = jnp.int32(0)
+        owners, values, codes = [], [], []
+        marks = jnp.int32(0)
         for f in range(GROUP):
             plan = plan_ref[g * GROUP + f]
             j = lax.shift_right_logical(plan, 12)
             r = lax.bitwise_and(plan, 4095)
-            count = jnp.where(g * GROUP + f < total_ref[0], counts_ref[j], 0)
             owners.append(j)
-            value = None
+            value = jnp.zeros((4, pts), jnp.float32)
             for v in range(PER):
                 code = codes_ref[r + v, j]
-                device = lax.shift_right_logical(code, 7)
-                run = runs_ref[device, lax.bitwise_and(code, 127)]
-                length = jnp.where(r + v < count, lax.bitwise_and(run, 4095), 0)
-                start = lax.shift_right_logical(run, 12)
-                longest = jnp.maximum(longest, length)
-                part = piece(device, start, jnp.minimum(length, CHUNK), v)
-                value = part if value is None else value + part
-                runs.append((device, start, length, j))
+                word = words_ref[code]
+                left = v * CHUNK
+                moved = window(
+                    lax.shift_right_logical(word, 16),
+                    lax.bitwise_and(lax.shift_right_logical(word, 8), 127),
+                    left,
+                )
+                right = left + lax.bitwise_and(word, 63)
+                fresh = jnp.where(lane < right, moved, 0.0)
+                value = fresh if v == 0 else jnp.where(lane < left, value, fresh)
+                marks = lax.bitwise_or(marks, word)
+                codes.append(code)
             values.append(value)
         for f in range(GROUP):
             row = half * GROUP + f
             buffer[pl.ds(row * 4, 4), :] = values[f]
             owner_ref[row] = owners[f]
-        return longest, runs
-
-    def note(longest, runs):
-        @pl.when(longest > CHUNK)
+        return marks, codes, owners
+
+    def note(fresh, marks, codes, owners):
+        @pl.when(fresh & (lax.bitwise_and(marks, LONG) > 0))
         def _():
-            for device, start, length, j in runs:
-
-                @pl.when(length > CHUNK)
+            for n, code in enumerate(codes):
+
+                @pl.when(lax.bitwise_and(words_ref[code], LONG) > 0)
                 def _():
                     at = extra_ref[0]
-                    extra_run[at] = start * 4096 + length
-                    extra_from[at] = device * 4096 + j
+                    extra_code[at] = code
+                    extra_owner[at] = owners[n // PER]
                     extra_ref[0] = at + 1
 
     def flush(half):
@@ -634,15 +635,15 @@
             coefs_ref[at, :] = coefs_ref[at, :] + sums[f][0:YR]
 
     groups = (total_ref[0] + (GROUP - 1)) // GROUP
-    note(*collect(0, 0))
+    note(groups > 0, *collect(0, 0))
 
     @pl.loop(0, groups)
     def _(g):
         half = lax.bitwise_and(g, 1)
         later = jnp.minimum(g + 1, groups - 1)
-        longest, runs = collect(later, 1 - half)
+        found = collect(later, 1 - half)
         flush(half)
-        note(jnp.where(later > g, longest, 0), runs)
+        note(later > g, *found)
 
     @pl.when(extra_ref[0] > 0)
     def _():
@@ -651,17 +652,20 @@
 
         @pl.loop(0, extra_ref[0])
         def _(n):
-            run, source = extra_run[n], extra_from[n]
-            device, j = lax.shift_right_logical(source, 12), lax.bitwise_and(source, 4095)
+            code = extra_code[n]
+            device = lax.shift_right_logical(code, 7)
+            run = runs_ref[device, lax.bitwise_and(code, 127)]
             start = lax.shift_right_logical(run, 12) + CHUNK
             length = lax.bitwise_and(run, 4095) - CHUNK
 
             @pl.loop(0, lax.shift_right_logical(length + (pts - 1), 7))
             def _(c):
                 row = extra_ref[1]
-                part = piece(device, start + c * pts, jnp.minimum(length - c * pts, pts), 0)
-                buffer[pl.ds(row * 4, 4), :] = part
-                owner_ref[row] = j
+                place = start + c * pts
+                tile = device * held + lax.shift_right_logical(place, 7)
+                moved = window(tile, lax.bitwise_and(place, 127), 0)
+                buffer[pl.ds(row * 4, 4), :] = jnp.where(lane < length - c * pts, moved, 0.0)
+                owner_ref[row] = extra_owner[n]
                 extra_ref[1] = row + 1
 
                 @pl.when(row + 1 == GROUP)
@@ -710,17 +714,18 @@
     value = index[None, :] * 4096 + (block - starts[None, :]) * PER
     plan = jnp.sum(jnp.where(inside, value, 0), axis=1)
     total = ends[listed - 1]
+    plan = jnp.where(block[:, 0] < total, plan, devices)
     return total.reshape(1).astype(jnp.int32), plan.astype(jnp.int32)
 
 
-def project(counts, codes, runs, blocks, tables, green):
-    listed = counts.shape[0]
+def project(counts, codes, words, runs, blocks, tables, green):
+    lists, listed = runs.shape
     pts = tables[0].shape[1]
     smem = pl.BlockSpec(memory_space=pltpu.SMEM)
     vmem = pl.BlockSpec(memory_space=pltpu.VMEM)
-    total, plan = block_plan(counts, codes.shape[0])
+    total, plan = block_plan(counts, lists)
     return pl.pallas_call(
-        project_kernel,
+        functools.partial(project_kernel, lists),
         out_shape=jax.ShapeDtypeStruct((listed, HP, NRAD), jnp.bfloat16),
         in_specs=[smem] * 5 + [vmem] * 4,
         out_specs=vmem,
@@ -736,30 +741,34 @@
         ],
         compiler_params=pltpu.CompilerParams(vmem_limit_bytes=40 << 20),
         name="project",
-    )(total, plan, counts, codes, runs, blocks, *tables, green)
-
-
-def scatter_kernel(blocks_ref, lists_ref, rows_at, out_ref, acc_ref):
-    devices, _, _, listed = blocks_ref.shape
+    )(total, plan, codes, words.reshape(-1), runs, blocks, *tables, green)
+
+
+def scatter_kernel(
+    lists_ref, blocks_ref, atoms_ref, mine_ref, places_ref, out_ref, info_ref, words_ref, runs_ref, acc_ref
+):
+    devices, listed = atoms_ref.shape
+    held = blocks_ref.shape[0] // lists_ref
     wide = 256
     acc_ref[...] = jnp.zeros_like(acc_ref)
     column = lax.broadcasted_iota(jnp.int32, (wide, listed), 0)
     groups = acc_ref.shape[0] // 32
-
     steps = 8
 
     @pl.loop(0, devices // steps)
     def _(g):
         total = acc_ref[...]
+        packed = []
         for v in range(0, steps, 2):
             targets, parts = [], []
             for q in (g * steps + v, g * steps + v + 1):
-                ids = lists_ref[pl.ds(q, 1), :]
+                ids = atoms_ref[pl.ds(q, 1), :]
                 targets.append(
                     (column == lax.bitwise_and(ids, wide - 1)).astype(jnp.bfloat16)
                 )
                 group = lax.shift_right_logical(ids, 8)
-                tiles = [blocks_ref[q, rows_at + m] for m in range(3)]
+                tiles = [blocks_ref[(q + 1) * held - 3 + m] for m in range(3)]
+                packed.append(tiles[0][0:1])
                 mom = jnp.concatenate(tiles + [jnp.zeros((4, listed), jnp.float32)], axis=0)
                 top = mom.astype(jnp.bfloat16).astype(jnp.float32)
                 both = [
@@ -775,21 +784,45 @@
                 preferred_element_type=jnp.float32,
             )
         acc_ref[...] = total
-
+        at = pl.ds(pl.multiple_of(g * steps, steps), steps)
+        run = jnp.concatenate(packed, axis=0).astype(jnp.int32)
+        runs_ref[at, :] = run
+        start, length = lax.shift_right_logical(run, 12), lax.bitwise_and(run, 4095)
+        device = g * steps + lax.broadcasted_iota(jnp.int32, (steps, listed), 0)
+        tile = device * held + lax.shift_right_logical(start, 7)
+        word = tile * 65536 + lax.bitwise_and(start, 127) * 256 + jnp.minimum(length, CHUNK)
+        words_ref[at, :] = word + jnp.where(length > CHUNK, LONG, 0)
+
+    words_ref[devices : devices + 8, :] = jnp.zeros((8, listed), jnp.int32)
+    mine = jnp.zeros((16, listed), jnp.float32)
     for h in range(groups):
-        out_ref[:, h * wide : (h + 1) * wide] = (
-            acc_ref[h * 32 + 1 : h * 32 + 10, :] + acc_ref[h * 32 + 17 : h * 32 + 26, :]
+        both = acc_ref[h * 32 : h * 32 + 16, :] + acc_ref[h * 32 + 16 : h * 32 + 32, :]
+        out_ref[:, h * wide : (h + 1) * wide] = both[1:10]
+        mine = mine + jnp.dot(
+            both,
+            (column + h * wide == mine_ref[...]).astype(jnp.float32),
+            precision=lax.Precision.HIGHEST,
+            preferred_element_type=jnp.float32,
         )
-
-
-def scatter_moments(blocks, lists, atoms):
+    info_ref[...] = jnp.zeros_like(info_ref)
+    info_ref[0:3, :] = places_ref[...]
+    info_ref[3:12, :] = mine[1:10]
+
+
+def scatter_moments(blocks, lists, my_list, places, atoms):
+    devices, listed = lists.shape
     return pl.pallas_call(
-        lambda b, l, o, a: scatter_kernel(b, l, blocks.shape[1] - 3, o, a),
-        out_shape=jax.ShapeDtypeStruct((9, atoms), jnp.float32),
+        functools.partial(scatter_kernel, devices),
+        out_shape=(
+            jax.ShapeDtypeStruct((9, atoms), jnp.float32),
+            jax.ShapeDtypeStruct((16, listed), jnp.float32),
+            jax.ShapeDtypeStruct((devices + 8, listed), jnp.int32),
+            jax.ShapeDtypeStruct((devices, listed), jnp.int32),
+        ),
         scratch_shapes=[pltpu.VMEM((atoms // 256 * 32, 256), jnp.float32)],
         compiler_params=pltpu.CompilerParams(vmem_limit_bytes=40 << 20),
         name="scatter_moments",
-    )(blocks, lists)
+    )(blocks, lists, my_list.reshape(1, listed), places)
 
 
 def entry_tables(lists, my_list):
@@ -806,8 +839,11 @@
     ).astype(jnp.int32)
     rank = jnp.where(present, rank, devices)
     code = order[:, None].astype(jnp.int32) * listed + held - 1
-    picked = rank[None, :, :] == order[:, None, None]
-    codes = jnp.sum(jnp.where(picked, code[None], 0), axis=1)
+    row = jnp.arange(devices + 8)
+    picked = rank[None, :, :] == row[:, None, None]
+    picked = picked & present[None, :, :]
+    none = devices * listed
+    codes = none + jnp.sum(jnp.where(picked, code[None] - none, 0), axis=1)
     return jnp.sum(present.astype(jnp.int32), axis=0), codes
 
 
@@ -833,13 +869,10 @@
     places = atom_pos[:, my_list]
     mine = point_blocks(grid_points, weighted_density, point_slot, places, tables, moment_table)
     gathered = gather_blocks(mine)
-    blocks = gathered.reshape((devices,) + mine.shape)
+    blocks = gathered.reshape((devices * mine.shape[0],) + mine.shape[1:])
     counts, codes = entry_tables(lists, my_list)
-    runs = blocks[:, mine.shape[0] - 3, 0, :].astype(jnp.int32)
-    slot_pot = project(counts, codes, runs, blocks, tables, green)
-    moments = scatter_moments(blocks, lists, atoms)
-    slot_table = jnp.concatenate([places, moments[:, my_list]], axis=0).T
-    slot_table = jnp.pad(slot_table, ((0, 0), (0, 128 - slot_table.shape[1])))
+    moments, slot_table, words, runs = scatter_moments(blocks, lists, my_list, places, atoms)
+    slot_pot = project(counts, codes, words, runs, blocks, tables, green)
     return evaluate(
         grid_points, near_slot, slot_table, slot_pot, atom_pos, moments, decay_rates
     )

time: 149 us -> 135 us (0.906)
  Pallas kernels: 128 us -> 116 us
  local copies, waits for them, and re-layouts: 10.8 us -> 8.52 us
    pallas_call x2, Pallas kernels: 56.3 us -> 44.1 us  [the longest x1 37.9 us: project(): pl.pallas_call(functools.partial(project_kernel, lists), out_shape=jax.Sh...]
    unnamed x20 -> x23, local copies, waits for them, and re-layouts: 5.76 us -> 6.41 us
where the time goes in v4:
time: 135 us; the launch traced here: 134 us
  Pallas kernels  116 us (86%)
  other arithmetic  9.33 us (7%)
  local copies, waits for them, and re-layouts  8.52 us (6%)
    pallas_call x1, Pallas kernels, project(): pl.pallas_call(functools.partial(project_kernel, lists), out_shape=jax.Sh...  37.9 us
    pallas_call x1, Pallas kernels, evaluate(): pl.pallas_call(evaluate_kernel, out_shape=jax.ShapeDtypeStruct((batches,...  34.4 us
    pallas_call x1, Pallas kernels, gather_blocks(): pl.pallas_call(functools.partial(gather_kernel, cuts), out_shape=jax.Shap...  30.5 us
    pallas_call x1, Pallas kernels, point_blocks(): pl.pallas_call(point_blocks_kernel, out_shape=jax.ShapeDtypeStruct((rows,...  6.68 us
    unnamed x23, local copies, waits for them, and re-layouts  6.41 us
    pallas_call x1, Pallas kernels, scatter_moments(): pl.pallas_call(functools.partial(scatter_kernel, devices), out_shape=(jax...  6.26 us
    reduce_sum x1, other arithmetic, entry_tables(): held = jnp.sum(jnp.where(same, slot, 0), axis=1)  4.05 us

profile of v4, /device:TPU:1, one launch (start us, length us, event | category | flops | bytes accessed | tf_op | source)
XLA Modules:
  0.0 133.9 jit_solution(8667326762261307450)
XLA Ops:
  0.0 0.7 broadcast_multiply_fusion
  0.7 0.7 fusion.4
  1.4 0.1 broadcast_in_dim.53.first_ref
  1.5 0.1 broadcast_in_dim.55.rate_ref
  1.5 4.1 %select_reduce_fusion.1 = s32[128,128]{1,0:T(8,128)S(1)} fusion(s32[128]{0:T(128)S(1)} %iota_add_fusion, s32[128]{0:T(128)S(1)} %bitcast.28, s32[128,128]{1,0:T(8,128)} %bitcast.20), kind=kLoop, calls=%fused_computation.4 | loop fusion | flops 6275072 | bytes 132096 | tf_op jit(solution)/shard_map/reduce_sum | solution.py:832
  5.6 0.1 convert_reduce_fusion
  5.7 0.1 select_reduce_fusion.3
  5.8 0.6 slice.12.total_ref
  6.4 0.7 select_reduce_fusion.2
  7.1 0.6 fusion.3.plan_ref
  7.8 0.1 fusion.2
  7.9 2.3 %select_reduce_fusion = s32[136,128]{1,0:T(8,128)S(1)} fusion(s32[128,128]{1,0:T(8,128)S(1)} %get-tuple-element.17, s32[128,128]{1,0:T(8,128)S(1)} %fusion.2, pred[128,128]{1,0:T(8,128)(4,1)S(1)} %bitcast.29), kind=kLoop, calls=%fused_computation.1 | loop fusion | flops 8895488 | bytes 217088 | tf_op jit(solution)/shard_map/reduce_sum | solution.py:846
  10.3 1.1 copy.12
  11.4 0.7 gather_fusion
  12.0 0.1 copy.13
  12.1 0.0 copy-start.5
  12.1 0.8 copy-done.5
  12.9 0.0 copy-start.8
  12.9 0.7 copy-done.8
  13.6 0.0 copy-start.9
  13.6 0.7 copy-done.9
  14.3 0.0 copy-start.10
  14.3 0.7 copy-done.10
  15.0 6.7 %point_blocks.1 = f32[76,128]{1,0:T(8,128)S(1)} custom-call(f32[3,2048]{1,0:T(4,128)S(1)} %copy-done.5, f32[1,2048]{1,0:T(1,128)S(1)} %bitcast.26, s32[1,2048]{1,0:T(1,128)S(1)} %bitcast.27, f32[3,128]{1,0:T(4,128)S(1)} %bitcast.24, f32[16,128]{1,0:T(8,128)S(1)} %broadcast_in_dim.53.first_ref, f32[128,128]{1,0:T(8,128)S(1)} %broadcast_in_dim.55.rate_ref, ...), custom_call_target="tpu_custom_call" | custom-call | tf_op jit(solution)/shard_map/point_blocks/pallas_call | solution.py:404
  21.6 0.7 reshape.119.mine_ref
  22.3 0.0 copy-start.3
  22.3 0.0 copy-start.2
  22.3 30.5 %gather_blocks.1 = f32[4,2,4,4,19,4,128]{6,5,4,3,2,1,0:T(4,128)} custom-call(f32[19,4,128]{2,1,0:T(4,128)} %reshape.119.mine_ref), custom_call_target="tpu_custom_call" | custom-call | tf_op jit(solution)/shard_map/gather_blocks/pallas_call | solution.py:510
  52.8 0.0 copy-done.3
  52.8 0.0 copy-start
  52.8 2.4 %copy-done = f32[4,2,4,4,19,4,128]{6,5,4,3,2,1,0:T(4,128)S(1)} copy-done((f32[4,2,4,4,19,4,128]{6,5,4,3,2,1,0:T(4,128)S(1)}, f32[4,2,4,4,19,4,128]{6,5,4,3,2,1,0:T(4,128)}, u32[]{:S(2)}) %copy-start) | copy-done | bytes 4980760
  55.2 0.0 copy-start.1
  55.2 6.3 %scatter_moments.1 = (f32[9,2048]{1,0:T(8,128)S(1)}, f32[16,128]{1,0:T(8,128)S(1)}, s32[136,128]{1,0:T(8,128)S(1)}, s32[128,128]{1,0:T(8,128)S(1)}) custom-call(f32[2432,4,128]{2,1,0:T(4,128)S(1)} %bitcast.17, s32[128,128]{1,0:T(8,128)S(1)} %bitcast.21, s32[1,128]{1,0:T(1,128)S(1)} %get-tuple-element.16.mine_ref, f32[3,128]{1,0:T(4,128)S(1)} %bitcast.25), custom_call_target="tpu_custom_call" | custom-call | tf_op jit(solution)/shard_map/scatter_moments/pallas_call | solution.py:814
  61.5 0.0 copy-done.2
  61.5 0.0 copy-done.1
  61.5 0.0 copy-start.4
  61.5 0.0 copy-start.6
  61.5 0.0 copy-start.7
  61.5 37.9 %project.1.slot_pot_ref = bf16[128,64,128]{2,1,0:T(8,128)(2,1)S(1)} custom-call(s32[1]{0:T(128)} %slice.12.total_ref, s32[4112]{0:T(1024)S(1)} %fusion.3.plan_ref, s32[136,128]{1,0:T(8,128)S(1)} %broadcast_add_fusion.codes_ref, s32[17408]{0:T(1024)S(1)} %bitcast.22, s32[128,128]{1,0:T(8,128)S(1)} %get-tuple-element.11.runs_ref, ...), custom_call_target="tpu_custom_call" | custom-call | tf_op jit(solution)/shard_map/project/pallas_call | solution.py:727
  99.4 0.0 copy-done.4
  99.4 0.0 copy-done.6
  99.4 0.0 copy-done.7
  99.4 34.4 %evaluate.1 = f32[16,1,128]{2,1,0:T(1,128)} custom-call(s32[16,64]{1,0:T(8,128)S(1)} %copy-done.7, s32[16,1,64]{2,1,0:T(1,128)S(1)} %bitcast.23, f32[3,2048]{1,0:T(4,128)S(1)} %copy-done.6, f32[16,128]{1,0:T(8,128)S(1)} %get-tuple-element.9.slot_table_ref, bf16[128,64,128]{2,1,0:T(8,128)(2,1)S(1)} %project.1.slot_pot_ref, f32[3,2048]{1,0:T(4,128)S(1)} %copy-done.4, ...), custom_call_target="tpu_custom_call" | custom-call | tf_op jit(solution)/shard_map/evaluate/pallas_call | solution.py:264
  (8 shorter events, 0.1 us)
Async XLA Ops:
  12.1 0.8 copy-start.5
  12.9 0.7 copy-start.8
  13.6 0.7 copy-start.9
  14.3 0.7 copy-start.10
  22.3 30.5 %copy-start.3 = (s32[16384]{0:T(1024)S(1)}, s32[16384]{0:T(1024)}, u32[]{:S(2)}) copy-start(s32[16384]{0:T(1024)} %param.13) | copy-start | bytes 196612
  22.3 39.2 %copy-start.2 = (f32[7,128,128]{2,1,0:T(8,128)S(1)}, f32[7,128,128]{2,1,0:T(8,128)}, u32[]{:S(2)}) copy-start(f32[7,128,128]{2,1,0:T(8,128)} %green_ref.1) | copy-start | bytes 1376260
  52.8 2.4 %copy-start = (f32[4,2,4,4,19,4,128]{6,5,4,3,2,1,0:T(4,128)S(1)}, f32[4,2,4,4,19,4,128]{6,5,4,3,2,1,0:T(4,128)}, u32[]{:S(2)}) copy-start(f32[4,2,4,4,19,4,128]{6,5,4,3,2,1,0:T(4,128)} %gather_blocks.1) | copy-start | bytes 14942212
  55.2 6.3 %copy-start.1 = (f32[4,2,4,4,19,4,128]{6,5,4,3,2,1,0:T(4,128)S(1)}, f32[4,2,4,4,19,4,128]{6,5,4,3,2,1,0:T(4,128)}, u32[]{:S(2)}) copy-start(f32[4,2,4,4,19,4,128]{6,5,4,3,2,1,0:T(4,128)} %gather_blocks.1) | copy-start | bytes 14942212
  61.5 37.9 %copy-start.4 = (f32[3,2048]{1,0:T(4,128)S(1)}, f32[3,2048]{1,0:T(4,128)}, u32[]{:S(2)}) copy-start(f32[3,2048]{1,0:T(4,128)} %atoms_ref.1) | copy-start | bytes 73732
  61.5 37.9 %copy-start.6 = (f32[3,2048]{1,0:T(4,128)S(1)}, f32[3,2048]{1,0:T(4,128)}, u32[]{:S(2)}) copy-start(f32[3,2048]{1,0:T(4,128)} %points_ref.3) | copy-start | bytes 73732
  61.5 37.9 %copy-start.7 = (s32[16,64]{1,0:T(8,128)S(1)}, s32[16,64]{1,0:T(8,128)}, u32[]{:S(2)}) copy-start(s32[16,64]{1,0:T(8,128)} %near_smem.1) | copy-start | bytes 12292

commit v5 on v4

--- a/solution.py
+++ b/solution.py
@@ -306,6 +306,53 @@
     return out.reshape(-1)
 
 
+def entry_tables(lists_ref, mine_ref, codes_ref, plan_ref, held_ref):
+    devices, listed = lists_ref.shape
+    shape = (listed, listed)
+    row = lax.broadcasted_iota(jnp.int32, shape, 0)
+    column = lax.broadcasted_iota(jnp.int32, shape, 1)
+    turned = lists_ref[...].astype(jnp.float32).T
+    mine = mine_ref[...].astype(jnp.float32)
+    slot = (row + 1).astype(jnp.float32)
+    for q in range(devices):
+        same = turned[:, q : q + 1] == mine
+        held_ref[q : q + 1, :] = jnp.sum(jnp.where(same, slot, 0.0), axis=0, keepdims=True)
+    held = held_ref[...]
+    present = jnp.where(held > 0.0, 1.0, 0.0).astype(jnp.bfloat16)
+    rank = jnp.dot(
+        (column < row).astype(jnp.bfloat16), present, preferred_element_type=jnp.float32
+    )
+    rank = jnp.where(held > 0.0, rank, 4096.0)
+    none = float(devices * listed)
+    code = (row * listed).astype(jnp.float32) + held - (1.0 + none)
+    for r in range(codes_ref.shape[0]):
+        picked = jnp.sum(jnp.where(rank == float(r), code, 0.0), axis=0, keepdims=True)
+        codes_ref[r : r + 1, :] = (picked + none).astype(jnp.int32)
+    counts = lax.dot_general(
+        present,
+        jnp.ones(shape, jnp.bfloat16),
+        (((0,), (0,)), ((), ())),
+        preferred_element_type=jnp.float32,
+    ).astype(jnp.int32)
+    needed = lax.shift_right_logical(counts + (PER - 1), 2)
+    ends = jnp.dot(
+        (column <= row).astype(jnp.bfloat16),
+        needed.astype(jnp.float32).astype(jnp.bfloat16),
+        preferred_element_type=jnp.float32,
+    ).astype(jnp.int32)
+    starts = ends - needed
+    total = ends[listed - 1 : listed, :]
+    last = plan_ref.shape[0] - 1
+    for m in range(last):
+        block = column + m * listed
+        inside = (block >= starts) & (block < ends)
+        value = jnp.sum(
+            jnp.where(inside, row * 4096 + (block - starts) * PER, 0), axis=0, keepdims=True
+        )
+        plan_ref[m : m + 1, :] = value + jnp.where(block[0:1, :] >= total, devices, 0)
+    plan_ref[last : last + 1, :] = total
+
+
 def point_blocks_kernel(
     points_ref,
     density_ref,
@@ -314,9 +361,15 @@
     first_ref,
     rate_ref,
     table_ref,
+    lists_ref,
+    mine_ref,
     out_ref,
+    codes_ref,
+    plan_ref,
     four_ref,
     q_rows,
+    held_ref,
+    sorted_ref,
 ):
     listed = places_ref.shape[1]
     pts = first_ref.shape[1]
@@ -391,20 +444,34 @@
             precision=lax.Precision.HIGHEST,
             preferred_element_type=jnp.float32,
         )
-    out_ref[0 : 4 * blocks, :] = sorted_rows
-    out_ref[4 * blocks : 4 * blocks + 1, :] = packed.T[0:1, :]
-    out_ref[4 * blocks + 1 : 4 * blocks + 10, :] = moments[0:9]
-    out_ref[4 * blocks + 10 : 4 * blocks + 12, :] = jnp.zeros((2, listed), jnp.float32)
-
-
-def point_blocks(points, density, slots, places, tables, moment_table):
+    sorted_ref[0 : 4 * blocks, :] = sorted_rows
+    sorted_ref[4 * blocks : 4 * blocks + 1, :] = packed.T[0:1, :]
+    sorted_ref[4 * blocks + 1 : 4 * blocks + 10, :] = moments[0:9]
+    sorted_ref[4 * blocks + 10 : 4 * blocks + 12, :] = jnp.zeros((2, listed), jnp.float32)
+    for m in range(blocks + 3):
+        out_ref[m] = sorted_ref[4 * m : 4 * m + 4, :]
+    entry_tables(lists_ref, mine_ref, codes_ref, plan_ref, held_ref)
+
+
+def point_blocks(points, density, slots, places, tables, moment_table, lists, my_list):
     count = points.shape[1]
+    devices, listed = lists.shape
     pts = tables[0].shape[1]
-    rows = 4 * (count // pts) + 12
-    out = pl.pallas_call(
+    tiles = count // pts + 3
+    plans = (listed * (devices // PER) + GROUP + listed - 1) // listed + 1
+    return pl.pallas_call(
         point_blocks_kernel,
-        out_shape=jax.ShapeDtypeStruct((rows, pts), jnp.float32),
-        scratch_shapes=[pltpu.VMEM((8, pts), jnp.float32), pltpu.VMEM((16, pts), jnp.float32)],
+        out_shape=(
+            jax.ShapeDtypeStruct((tiles, 4, pts), jnp.float32),
+            jax.ShapeDtypeStruct((devices + 8, listed), jnp.int32),
+            jax.ShapeDtypeStruct((plans, listed), jnp.int32),
+        ),
+        scratch_shapes=[
+            pltpu.VMEM((8, pts), jnp.float32),
+            pltpu.VMEM((16, pts), jnp.float32),
+            pltpu.VMEM((devices, listed), jnp.float32),
+            pltpu.VMEM((4 * tiles, pts), jnp.float32),
+        ],
         compiler_params=pltpu.CompilerParams(vmem_limit_bytes=40 << 20),
         name="point_blocks",
     )(
@@ -414,8 +481,9 @@
         places,
         *tables,
         moment_table,
-    )
-    return out.reshape(rows // 4, 4, pts)
+        lists,
+        my_list.reshape(1, listed),
+    )
 
 
 MESH = pl.DeviceIdType.MESH
@@ -527,12 +595,11 @@
 CHUNK = 32
 PER = 4
 LONG = 64
-GROUP = 16
+GROUP = 32
 
 
 def project_kernel(
     lists,
-    total_ref,
     plan_ref,
     codes_ref,
     words_ref,
@@ -634,7 +701,7 @@
             at = pl.ds(pl.multiple_of(owner_ref[half * GROUP + f] * YR, 8), YR)
             coefs_ref[at, :] = coefs_ref[at, :] + sums[f][0:YR]
 
-    groups = (total_ref[0] + (GROUP - 1)) // GROUP
+    groups = (plan_ref[plan_ref.shape[0] - first_ref.shape[1]] + (GROUP - 1)) // GROUP
     note(groups > 0, *collect(0, 0))
 
     @pl.loop(0, groups)
@@ -702,32 +769,15 @@
             ).astype(jnp.bfloat16)
 
 
-def block_plan(counts, devices):
-    listed = counts.shape[0]
-    index = jnp.arange(listed)
-    needed = (counts + (PER - 1)) // PER
-    ends = jnp.sum(jnp.where(index[None, :] <= index[:, None], needed[None, :], 0), axis=1)
-    starts = ends - needed
-    most = listed * (devices // PER) + GROUP
-    block = jnp.arange(most)[:, None]
-    inside = (block >= starts[None, :]) & (block < ends[None, :])
-    value = index[None, :] * 4096 + (block - starts[None, :]) * PER
-    plan = jnp.sum(jnp.where(inside, value, 0), axis=1)
-    total = ends[listed - 1]
-    plan = jnp.where(block[:, 0] < total, plan, devices)
-    return total.reshape(1).astype(jnp.int32), plan.astype(jnp.int32)
-
-
-def project(counts, codes, words, runs, blocks, tables, green):
+def project(plan, codes, words, runs, blocks, tables, green):
     lists, listed = runs.shape
     pts = tables[0].shape[1]
     smem = pl.BlockSpec(memory_space=pltpu.SMEM)
     vmem = pl.BlockSpec(memory_space=pltpu.VMEM)
-    total, plan = block_plan(counts, lists)
     return pl.pallas_call(
         functools.partial(project_kernel, lists),
         out_shape=jax.ShapeDtypeStruct((listed, HP, NRAD), jnp.bfloat16),
-        in_specs=[smem] * 5 + [vmem] * 4,
+        in_specs=[smem] * 4 + [vmem] * 4,
         out_specs=vmem,
         scratch_shapes=[
             pltpu.VMEM((2 * GROUP * 4, pts), jnp.float32),
@@ -741,7 +791,7 @@
         ],
         compiler_params=pltpu.CompilerParams(vmem_limit_bytes=40 << 20),
         name="project",
-    )(total, plan, codes, words.reshape(-1), runs, blocks, *tables, green)
+    )(plan.reshape(-1), codes, words.reshape(-1), runs, blocks, *tables, green)
 
 
 def scatter_kernel(
@@ -825,28 +875,6 @@
     )(blocks, lists, my_list.reshape(1, listed), places)
 
 
-def entry_tables(lists, my_list):
-    devices, listed = lists.shape
-    same = lists[:, :, None] == my_list[None, None, :]
-    slot = jnp.arange(1, listed + 1, dtype=jnp.int32)[None, :, None]
-    held = jnp.sum(jnp.where(same, slot, 0), axis=1)
-    present = held > 0
-    order = jnp.arange(devices)
-    rank = jnp.dot(
-        (order[None, :] < order[:, None]).astype(jnp.bfloat16),
-        present.astype(jnp.bfloat16),
-        preferred_element_type=jnp.float32,
-    ).astype(jnp.int32)
-    rank = jnp.where(present, rank, devices)
-    code = order[:, None].astype(jnp.int32) * listed + held - 1
-    row = jnp.arange(devices + 8)
-    picked = rank[None, :, :] == row[:, None, None]
-    picked = picked & present[None, :, :]
-    none = devices * listed
-    codes = none + jnp.sum(jnp.where(picked, code[None] - none, 0), axis=1)
-    return jnp.sum(present.astype(jnp.int32), axis=0), codes
-
-
 def per_device(
     grid_points,
     weighted_density,
@@ -867,12 +895,13 @@
     pts = grid_points.shape[1] // near_slot.shape[0]
     tables = radial_tables(decay_rates, pts)
     places = atom_pos[:, my_list]
-    mine = point_blocks(grid_points, weighted_density, point_slot, places, tables, moment_table)
+    mine, codes, plan = point_blocks(
+        grid_points, weighted_density, point_slot, places, tables, moment_table, lists, my_list
+    )
     gathered = gather_blocks(mine)
     blocks = gathered.reshape((devices * mine.shape[0],) + mine.shape[1:])
-    counts, codes = entry_tables(lists, my_list)
     moments, slot_table, words, runs = scatter_moments(blocks, lists, my_list, places, atoms)
-    slot_pot = project(counts, codes, words, runs, blocks, tables, green)
+    slot_pot = project(plan, codes, words, runs, blocks, tables, green)
     return evaluate(
         grid_points, near_slot, slot_table, slot_pot, atom_pos, moments, decay_rates
     )

time: 135 us -> 128 us (0.948)
  other arithmetic: 9.33 us -> 1.39 us
    reduce_sum x5 -> x0, other arithmetic: 7.27 us -> none  [the longest x1 4.05 us: entry_tables(): held = jnp.sum(jnp.where(same, slot, 0), axis=1)]
    pallas_call x1, Pallas kernels: 6.68 us -> 8.51 us  [point_blocks(): pl.pallas_call(point_blocks_kernel, out_shape=(jax.ShapeDtypeStruct((tile...]
    unnamed x23 -> x27, local copies, waits for them, and re-layouts: 6.41 us -> 7.86 us
where the time goes in v5:
time: 128 us; the launch traced here: 127 us
  Pallas kernels  117 us (91%)
  local copies, waits for them, and re-layouts  8.71 us (7%)
  other arithmetic  1.39 us (1%)
    pallas_call x1, Pallas kernels, project(): pl.pallas_call(functools.partial(project_kernel, lists), out_shape=jax.Sh...  37.3 us
    pallas_call x1, Pallas kernels, evaluate(): pl.pallas_call(evaluate_kernel, out_shape=jax.ShapeDtypeStruct((batches,...  34.4 us
    pallas_call x1, Pallas kernels, gather_blocks(): pl.pallas_call(functools.partial(gather_kernel, cuts), out_shape=jax.Shap...  30.5 us
    pallas_call x1, Pallas kernels, point_blocks(): pl.pallas_call(point_blocks_kernel, out_shape=(jax.ShapeDtypeStruct((tile...  8.51 us
    unnamed x27, local copies, waits for them, and re-layouts  7.86 us
    pallas_call x1, Pallas kernels, scatter_moments(): pl.pallas_call(functools.partial(scatter_kernel, devices), out_shape=(jax...  6.26 us

profile of v5, /device:TPU:1, one launch (start us, length us, event | category | flops | bytes accessed | tf_op | source)
XLA Modules:
  0.0 127.3 jit_solution(4361531145487576827)
XLA Ops:
  0.0 0.0 copy-start.4
  0.0 0.7 broadcast_multiply_fusion
  0.7 0.7 fusion
  1.4 0.1 broadcast_in_dim.8.first_ref
  1.5 0.1 broadcast_in_dim.9.rate_ref
  1.5 1.1 copy.10
  2.7 0.6 gather_fusion
  3.3 0.1 copy.11
  3.4 0.0 copy-start.3
  3.4 0.9 copy-done.3
  4.2 0.0 copy-start.6
  4.3 0.8 copy-done.6
  5.0 0.0 copy-start.10
  5.0 0.7 copy-done.10
  5.7 0.0 copy-start.11
  5.7 0.7 copy-done.11
  6.4 0.0 copy-start.12
  6.4 0.7 copy-done.12
  7.1 8.5 %point_blocks.1 = (f32[19,4,128]{2,1,0:T(4,128)S(1)}, s32[136,128]{1,0:T(8,128)S(1)}, s32[34,128]{1,0:T(8,128)S(1)}) custom-call(f32[3,2048]{1,0:T(4,128)S(1)} %copy-done.6, f32[1,2048]{1,0:T(1,128)S(1)} %bitcast.24, s32[1,2048]{1,0:T(1,128)S(1)} %bitcast.25, f32[3,128]{1,0:T(4,128)S(1)} %bitcast.22, f32[16,128]{1,0:T(8,128)S(1)} %broadcast_in_dim.8.first_ref, ...), custom_call_target="tpu_custom_call" | custom-call | tf_op jit(solution)/shard_map/point_blocks/pallas_call | solution.py:462
  15.6 0.0 copy-start.8
  15.6 0.6 copy-done.8
  16.2 0.0 copy-start.2
  16.2 30.5 %gather_blocks.1 = f32[4,2,4,4,19,4,128]{6,5,4,3,2,1,0:T(4,128)} custom-call(f32[19,4,128]{2,1,0:T(4,128)} %copy-done.8), custom_call_target="tpu_custom_call" | custom-call | tf_op jit(solution)/shard_map/gather_blocks/pallas_call | solution.py:578
  46.7 0.0 copy-done.4
  46.7 0.0 copy-start
  46.7 2.4 %copy-done = f32[4,2,4,4,19,4,128]{6,5,4,3,2,1,0:T(4,128)S(1)} copy-done((f32[4,2,4,4,19,4,128]{6,5,4,3,2,1,0:T(4,128)S(1)}, f32[4,2,4,4,19,4,128]{6,5,4,3,2,1,0:T(4,128)}, u32[]{:S(2)}) %copy-start) | copy-done | bytes 4980760
  49.1 0.0 copy-start.1
  49.1 6.3 %scatter_moments.1 = (f32[9,2048]{1,0:T(8,128)S(1)}, f32[16,128]{1,0:T(8,128)S(1)}, s32[136,128]{1,0:T(8,128)S(1)}, s32[128,128]{1,0:T(8,128)S(1)}) custom-call(f32[2432,4,128]{2,1,0:T(4,128)S(1)} %bitcast.14, s32[128,128]{1,0:T(8,128)S(1)} %bitcast.18, s32[1,128]{1,0:T(1,128)S(1)} %get-tuple-element.20.mine_ref, f32[3,128]{1,0:T(4,128)S(1)} %bitcast.23), custom_call_target="tpu_custom_call" | custom-call | tf_op jit(solution)/shard_map/scatter_moments/pallas_call | solution.py:864
  55.4 0.0 copy-start.5
  55.4 0.0 copy-start.7
  55.4 0.0 copy-start.9
  55.4 0.0 copy-done.2
  55.4 0.0 copy-done.1
  55.4 37.3 %project.1.slot_pot_ref = bf16[128,64,128]{2,1,0:T(8,128)(2,1)S(1)} custom-call(s32[4352]{0:T(1024)S(1)} %bitcast.21, s32[136,128]{1,0:T(8,128)S(1)} %get-tuple-element.15.codes_ref, s32[17408]{0:T(1024)S(1)} %bitcast.19, s32[128,128]{1,0:T(8,128)S(1)} %get-tuple-element.17.runs_ref, f32[2432,4,128]{2,1,0:T(4,128)S(1)} %bitcast.15, ...), custom_call_target="tpu_custom_call" | custom-call | tf_op jit(solution)/shard_map/project/pallas_call | solution.py:777
  92.8 0.0 copy-done.5
  92.8 0.0 copy-done.7
  92.8 0.0 copy-done.9
  92.8 34.4 %evaluate.1 = f32[16,1,128]{2,1,0:T(1,128)} custom-call(s32[16,64]{1,0:T(8,128)S(1)} %copy-done.9, s32[16,1,64]{2,1,0:T(1,128)S(1)} %bitcast.20, f32[3,2048]{1,0:T(4,128)S(1)} %copy-done.7, f32[16,128]{1,0:T(8,128)S(1)} %get-tuple-element.13.slot_table_ref, bf16[128,64,128]{2,1,0:T(8,128)(2,1)S(1)} %project.1.slot_pot_ref, f32[3,2048]{1,0:T(4,128)S(1)} %copy-done.5, ...), custom_call_target="tpu_custom_call" | custom-call | tf_op jit(solution)/shard_map/evaluate/pallas_call | solution.py:264
  (2 shorter events, 0.0 us)
Async XLA Ops:
  0.0 46.7 %copy-start.4 = (s32[16384]{0:T(1024)S(1)}, s32[16384]{0:T(1024)}, u32[]{:S(2)}) copy-start(s32[16384]{0:T(1024)} %param.13) | copy-start | bytes 196612
  3.4 0.9 copy-start.3
  4.2 0.8 copy-start.6
  5.0 0.7 copy-start.10
  5.7 0.7 copy-start.11
  6.4 0.7 copy-start.12
  15.6 0.6 copy-start.8
  16.2 39.2 %copy-start.2 = (f32[7,128,128]{2,1,0:T(8,128)S(1)}, f32[7,128,128]{2,1,0:T(8,128)}, u32[]{:S(2)}) copy-start(f32[7,128,128]{2,1,0:T(8,128)} %green_ref.1) | copy-start | bytes 1376260
  46.7 2.4 %copy-start = (f32[4,2,4,4,19,4,128]{6,5,4,3,2,1,0:T(4,128)S(1)}, f32[4,2,4,4,19,4,128]{6,5,4,3,2,1,0:T(4,128)}, u32[]{:S(2)}) copy-start(f32[4,2,4,4,19,4,128]{6,5,4,3,2,1,0:T(4,128)} %gather_blocks.1) | copy-start | bytes 14942212
  49.1 6.3 %copy-start.1 = (f32[4,2,4,4,19,4,128]{6,5,4,3,2,1,0:T(4,128)S(1)}, f32[4,2,4,4,19,4,128]{6,5,4,3,2,1,0:T(4,128)}, u32[]{:S(2)}) copy-start(f32[4,2,4,4,19,4,128]{6,5,4,3,2,1,0:T(4,128)} %gather_blocks.1) | copy-start | bytes 14942212
  55.4 37.4 %copy-start.5 = (f32[3,2048]{1,0:T(4,128)S(1)}, f32[3,2048]{1,0:T(4,128)}, u32[]{:S(2)}) copy-start(f32[3,2048]{1,0:T(4,128)} %atoms_ref.1) | copy-start | bytes 73732
  55.4 37.4 %copy-start.7 = (f32[3,2048]{1,0:T(4,128)S(1)}, f32[3,2048]{1,0:T(4,128)}, u32[]{:S(2)}) copy-start(f32[3,2048]{1,0:T(4,128)} %points_ref.3) | copy-start | bytes 73732
  55.4 37.4 %copy-start.9 = (s32[16,64]{1,0:T(8,128)S(1)}, s32[16,64]{1,0:T(8,128)}, u32[]{:S(2)}) copy-start(s32[16,64]{1,0:T(8,128)} %near_smem.1) | copy-start | bytes 12292
